TPU v7x, 256 devices: a whole 4x4x8 slice. The times are simulated.
256 devices in a mesh: ctx: 16 (over y, x), exp: 16 (over z, core).
Axes of the slice: x: 4, y: 4, z: 8, core: 2. Of those that a mesh axis runs over, the one named last changes fastest.
Arguments:
- tokens: bfloat16 [2048, 4096], P('ctx', 'exp'), may hold values from -6 to 6
- input_weight: bfloat16 [4096, 8192], P('ctx', 'exp'), may hold values from -0.09375 to 0.09375
- gate_weight: bfloat16 [4096, 8192], P('ctx', 'exp'), may hold values from -0.09375 to 0.09375
- conv_weight: float32 [4, 8192], P(None, 'exp'), may hold values from -3 to 3
- conv_bias: float32 [8192], P('exp'), may hold values from -3 to 3
- state_weight: bfloat16 [8192, 32], P('exp'), may hold values from -0.0078125 to 0.0078125
- step_size: float32 [2048, 8192], P('ctx', 'exp'), may hold values from 0 to 1, as said below
- skip_gain: float32 [8192], P('exp'), may hold values from 0.5 to 2
- output_weight: bfloat16 [8192, 4096], P('exp', 'ctx'), may hold values from -0.0625 to 0.0625
- norm_gain: float32 [4096], replicated, may hold values from 0.1 to 1.9
- router_weight: bfloat16 [4096, 16], replicated, may hold values from -0.09375 to 0.09375
- expert_gate: bfloat16 [16, 7168, 4096], P('exp', 'ctx'), may hold values from -0.09375 to 0.09375
- expert_up: bfloat16 [16, 7168, 4096], P('exp', 'ctx'), may hold values from -0.09375 to 0.09375
- expert_down: bfloat16 [16, 7168, 4096], P('exp', 'ctx'), may hold values from -0.0625 to 0.0625
- expert_ids: int32 [2048, 2], P(('ctx', 'exp')), may hold values from 0 to 15, all different within a row; in each aligned block of 8 rows (0 to 7, 8 to 15, ...) at most 2 rows name the same one
Outputs:
- layer_out: bfloat16 [2048, 4096], P(('ctx', 'exp'))
Inputs may be any that keep to these rules, and one draw needn't show every extreme that they name: `expert_ids`: each token names 2 different experts; in each aligned block of 8 tokens no expert is named by more than 2 tokens. `step_size`: a positive rate for each token and channel.
All inputs are finite; a program needn't handle non-finite values.
Results may differ from a plain program's by a relative error of at most 0.028.
Values may be sent and summed in bfloat16 or wider, within the bound.
A program may use at most 128 MiB of HBM per device.

v0:
```python
import jax
import jax.numpy as jnp
from jax import lax
from jax.sharding import PartitionSpec as P

STATE = 16
CONV = 4
TOP = 2
CAP = 2


precise = lax.Precision.HIGHEST


def shifted(shard, axis, by):
    devices = lax.axis_size(axis)
    pairs = [(i, i + by) for i in range(devices) if 0 <= i + by < devices]
    return lax.ppermute(shard, axis, pairs)


def causal_part(scores, decay_block, input_block):
    length = decay_block.shape[0]
    causal = (jnp.arange(length)[:, None] >= jnp.arange(length)[None, :])[:, :, None]
    distance = decay_block[:, None, :] - decay_block[None, :, :]
    weight = jnp.where(causal, jnp.exp(-jnp.where(causal, distance, 0.0)), 0.0)
    return jnp.einsum("ts,tsc,sc->tc", scores, weight, input_block, precision=precise)


def local(
    tokens,
    input_weight,
    gate_weight,
    conv_weight,
    conv_bias,
    state_weight,
    step_size,
    skip_gain,
    output_weight,
    norm_gain,
    router_weight,
    expert_gate,
    expert_up,
    expert_down,
    expert_ids,
):
    whole_stretch = lax.all_gather(tokens, "exp", axis=1, tiled=True)
    stretch_rows = whole_stretch.shape[0]
    inner_width = input_weight.shape[1]
    inner_x = jnp.dot(
        whole_stretch,
        lax.all_gather(input_weight, "ctx", axis=0, tiled=True),
        preferred_element_type=jnp.float32,
    )
    inner_z = jnp.dot(
        whole_stretch,
        lax.all_gather(gate_weight, "ctx", axis=0, tiled=True),
        preferred_element_type=jnp.float32,
    )
    inner_x = inner_x.astype(jnp.bfloat16)
    inner_z = inner_z.astype(jnp.bfloat16)
    earlier_rows = shifted(inner_x[stretch_rows - (CONV - 1) :], "ctx", 1)
    extended = jnp.concatenate([earlier_rows, inner_x], 0).astype(jnp.float32)
    filtered = jnp.broadcast_to(conv_bias[None, :], (stretch_rows, inner_width))
    for offset in range(CONV):
        filtered = (
            filtered + conv_weight[offset][None, :] * extended[offset : offset + stretch_rows]
        )
    mixer_in = jax.nn.silu(filtered).astype(jnp.bfloat16)
    mixer_wide = mixer_in.astype(jnp.float32)
    projections = lax.psum(
        jnp.dot(mixer_in, state_weight, preferred_element_type=jnp.float32), "exp"
    )
    input_gain = projections[:, :STATE]
    readout = projections[:, STATE:]
    cumulative = jnp.cumsum(step_size, 0)
    scores = jnp.dot(readout, input_gain.T, precision=precise)
    block_width = 128
    block_count = inner_width // block_width
    decay_blocks = cumulative.reshape(stretch_rows, block_count, block_width).transpose(1, 0, 2)
    incoming_slabs = mixer_wide.reshape(stretch_rows, block_count, block_width).transpose(1, 0, 2)
    inside = lax.map(
        lambda paired: causal_part(scores, paired[0], paired[1]), (decay_blocks, incoming_slabs)
    )
    inside = inside.transpose(1, 0, 2).reshape(stretch_rows, inner_width)
    total_decay = cumulative[stretch_rows - 1]
    tail_weight = jnp.exp(-(total_decay[None, :] - cumulative)) * mixer_wide
    local_end = jnp.dot(tail_weight.T, input_gain, precision=precise)
    stretch_keep = jnp.exp(-total_decay)

    def relay_step(turn_index, received):
        leaving = stretch_keep[:, None] * received + local_end
        return shifted(leaving, "ctx", 1)

    entering = lax.fori_loop(0, lax.axis_size("ctx") - 1, relay_step, jnp.zeros_like(local_end))
    carried = jnp.exp(-cumulative) * jnp.dot(readout, entering.T, precision=precise)
    mixed_state = (inside + carried + skip_gain[None, :] * mixer_wide) * jax.nn.silu(
        inner_z.astype(jnp.float32)
    )
    blender_result = mixed_state.astype(jnp.bfloat16)
    row_count = expert_ids.shape[0]
    start_row = lax.axis_index("exp") * row_count
    own_tokens = lax.dynamic_slice_in_dim(whole_stretch, start_row, row_count, 0)
    out_whole = lax.all_gather(output_weight, "ctx", axis=1, tiled=True)
    projected = lax.psum_scatter(
        jnp.dot(blender_result, out_whole, preferred_element_type=jnp.float32).astype(jnp.bfloat16),
        "exp",
        scatter_dimension=0,
        tiled=True,
    ).astype(jnp.float32)
    residual = (own_tokens.astype(jnp.float32) + projected).astype(jnp.bfloat16)
    stream = residual.astype(jnp.float32)
    normed = (
        stream
        * lax.rsqrt(jnp.mean(stream * stream, -1, keepdims=True) + 1e-05)
        * norm_gain[None, :]
    ).astype(jnp.bfloat16)
    logits = jnp.dot(normed, router_weight, preferred_element_type=jnp.float32)
    experts = router_weight.shape[1]
    expert_range = jnp.arange(experts, dtype=jnp.int32)
    chosen = expert_ids[:, :, None] == expert_range[None, None, :]
    selected_entry = jnp.sum(jnp.where(chosen, logits[:, None, :], 0.0), -1)
    shares = jax.nn.sigmoid(selected_entry - selected_entry[:, ::-1])
    flat_hits = chosen.reshape(row_count * TOP, experts).astype(jnp.int32)
    earlier_hits = jnp.cumsum(flat_hits, 0) - flat_hits
    slot_index = jnp.sum(earlier_hits * flat_hits, -1)
    target = expert_ids.reshape(-1) * CAP + slot_index
    placed = target[:, None] == jnp.arange(experts * CAP, dtype=jnp.int32)[None, :]
    placed = placed.reshape(row_count, TOP, experts * CAP)
    selector = jnp.any(placed, 1).astype(jnp.bfloat16)
    outgoing = lax.dot_general(
        selector, normed, (((0,), (0,)), ((), ())), preferred_element_type=jnp.float32
    ).astype(jnp.bfloat16)
    outgoing = outgoing.reshape(experts, CAP, -1)
    arrived = lax.all_to_all(outgoing, "exp", split_axis=0, concat_axis=0, tiled=True)
    arrived = arrived.reshape(-1, arrived.shape[2])
    gate_part = expert_gate[0]
    up_part = expert_up[0]
    down_part = expert_down[0]
    shard_rows = lax.all_gather(arrived, "ctx", axis=0, tiled=True)
    gate_value = lax.dot_general(
        shard_rows, gate_part, (((1,), (1,)), ((), ())), preferred_element_type=jnp.float32
    )
    up_value = lax.dot_general(
        shard_rows, up_part, (((1,), (1,)), ((), ())), preferred_element_type=jnp.float32
    )
    hidden = (jax.nn.silu(gate_value) * up_value).astype(jnp.bfloat16)
    partial_out = jnp.dot(hidden, down_part, preferred_element_type=jnp.float32)
    finished = lax.psum_scatter(
        partial_out.astype(jnp.bfloat16), "ctx", scatter_dimension=0, tiled=True
    )
    returned = lax.all_to_all(
        finished.reshape(experts, CAP, -1), "exp", split_axis=0, concat_axis=0, tiled=True
    )
    returned = returned.reshape(experts * CAP, -1).astype(jnp.float32)
    combine = jnp.sum(jnp.where(placed, shares[:, :, None], 0.0), 1)
    moe_out = jnp.dot(combine, returned, precision=precise)
    return (stream + moe_out).astype(jnp.bfloat16)


def solution(mesh):
    in_specs = (
        P("ctx", "exp"),
        P("ctx", "exp"),
        P("ctx", "exp"),
        P(None, "exp"),
        P("exp"),
        P("exp", None),
        P("ctx", "exp"),
        P("exp"),
        P("exp", "ctx"),
        P(),
        P(),
        P("exp", "ctx", None),
        P("exp", "ctx", None),
        P("exp", "ctx", None),
        P(("ctx", "exp"), None),
    )
    out_specs = P(("ctx", "exp"), None)
    return jax.shard_map(local, mesh=mesh, in_specs=in_specs, out_specs=out_specs, check_vma=False)
```

profile of v0, /device:TPU:1, one launch (start us, length us, event | category | flops | bytes accessed | tf_op | source)
XLA Modules:
  0.0 636.4 jit_solution(2759990935749958650)
XLA Ops:
  11.5 39.5 %all-gather.6.cloned.1.call-done = bf16[128,4096]{1,0:T(8,128)(2,1)} async-done(((bf16[128,256]{1,0:T(8,128)(2,1)}), bf16[128,4096]{1,0:T(8,128)(2,1)}) %all-gather.6.cloned.1.call-update) | async-done | bytes 1048592 | tf_op jit(solution)/shard_map/all_gather | solution.py:46
  51.0 57.7 %all-gather.8.cloned.1.call-done = bf16[4096,512]{1,0:T(8,128)(2,1)} async-done(((bf16[256,512]{1,0:T(8,128)(2,1)}), bf16[4096,512]{1,0:T(8,128)(2,1)}) %all-gather.8.cloned.1.call-update) | async-done | bytes 4194320 | tf_op jit(solution)/shard_map/all_gather | solution.py:51
  115.1 52.4 %all-gather.10.cloned.1.call-done = bf16[4096,512]{1,0:T(8,128)(2,1)} async-done(((bf16[256,512]{1,0:T(8,128)(2,1)}), bf16[4096,512]{1,0:T(8,128)(2,1)}) %all-gather.10.cloned.1.call-update) | async-done | bytes 4194320 | tf_op jit(solution)/shard_map/all_gather | solution.py:56
  170.7 46.7 %psum.7 = f32[128,32]{0,1:T(8,128)S(1)} all-reduce(f32[128,32]{0,1:T(8,128)S(1)} %fusion.54), channel_id=1, replica_groups=mesh['ctx'=16,'exp'=16] {'exp'}, use_global_device_ids=true, to_apply=%region_1.2 | all-reduce | flops 4096 | bytes 32768 | tf_op jit(solution)/shard_map/psum | solution.py:70
  218.1 39.1 %while.20 = (s32[]{:T(128)}, f32[4,128,128]{2,1,0:T(8,128)S(1)}, f32[4,128,128]{2,1,0:T(8,128)S(1)}, f32[4,128,128]{2,1,0:T(8,128)S(1)}, f32[128,128]{1,0:T(8,128)S(1)}, /*index=5*/s32[]{:T(128)}) while((s32[]{:T(128)}, f32[4,128,128]{2,1,0:T(8,128)S(1)}, f32[4,128,128]{2,1,0:T(8,128)S(1)}, f32[4,128,128]{2,1,0:T(8,128)S(1)}, ...), condition=%wide.region_3.4_spmd, body=%wide.region_2.3_spmd.sunk | while | flops 35667968 | bytes 688205 | solution.py:81
  218.1 9.7 %fusion.87 = f32[128,1,128]{2,1,0:T(1,128)S(1)} fusion(f32[128,128,1]{1,2,0:T(1,128)S(1)} %bitcast.88, f32[128,128]{1,0:T(8,128)S(1)} %get-tuple-element.140, f32[128,128]{1,0:T(8,128)S(1)} %get-tuple-element.141, pred[128,128]{1,0:T(8,128)(4,1)S(1)} %iota_compare_fusion.5), kind=kOutput, calls=%fused_computation.clone.1 | convolution fusion | flops 35651584 | bytes 278528 | tf_op jit(solution)/shard_map/while/body/eval_jaxpr/ts,tsc,sc->tc/dot_general | solution.py:26
  227.9 9.7 %fusion.87 = f32[128,1,128]{2,1,0:T(1,128)S(1)} fusion(f32[128,128,1]{1,2,0:T(1,128)S(1)} %bitcast.88, f32[128,128]{1,0:T(8,128)S(1)} %get-tuple-element.140, f32[128,128]{1,0:T(8,128)S(1)} %get-tuple-element.141, pred[128,128]{1,0:T(8,128)(4,1)S(1)} %iota_compare_fusion.5), kind=kOutput, calls=%fused_computation.clone.1 | convolution fusion | flops 35651584 | bytes 278528 | tf_op jit(solution)/shard_map/while/body/eval_jaxpr/ts,tsc,sc->tc/dot_general | solution.py:26
  237.6 9.7 %fusion.87 = f32[128,1,128]{2,1,0:T(1,128)S(1)} fusion(f32[128,128,1]{1,2,0:T(1,128)S(1)} %bitcast.88, f32[128,128]{1,0:T(8,128)S(1)} %get-tuple-element.140, f32[128,128]{1,0:T(8,128)S(1)} %get-tuple-element.141, pred[128,128]{1,0:T(8,128)(4,1)S(1)} %iota_compare_fusion.5), kind=kOutput, calls=%fused_computation.clone.1 | convolution fusion | flops 35651584 | bytes 278528 | tf_op jit(solution)/shard_map/while/body/eval_jaxpr/ts,tsc,sc->tc/dot_general | solution.py:26
  247.4 9.7 %fusion.87 = f32[128,1,128]{2,1,0:T(1,128)S(1)} fusion(f32[128,128,1]{1,2,0:T(1,128)S(1)} %bitcast.88, f32[128,128]{1,0:T(8,128)S(1)} %get-tuple-element.140, f32[128,128]{1,0:T(8,128)S(1)} %get-tuple-element.141, pred[128,128]{1,0:T(8,128)(4,1)S(1)} %iota_compare_fusion.5), kind=kOutput, calls=%fused_computation.clone.1 | convolution fusion | flops 35651584 | bytes 278528 | tf_op jit(solution)/shard_map/while/body/eval_jaxpr/ts,tsc,sc->tc/dot_general | solution.py:26
  257.1 90.6 %while.21 = (s32[]{:T(128)}, f32[512,16]{0,1:T(8,128)S(1)}, f32[512]{0:T(512)S(1)}, f32[512,16]{0,1:T(8,128)S(1)}, s32[]{:T(128)}) while((s32[]{:T(128)}, f32[512,16]{0,1:T(8,128)S(1)}, f32[512]{0:T(512)S(1)}, f32[512,16]{0,1:T(8,128)S(1)}, s32[]{:T(128)}) %tuple.40), condition=%wide.region_5.6_spmd, body=%wide.region_4.5_spmd.sunk | while | flops 16386 | bytes 231525 | solution.py:94
  280.0 5.8 collective-permute-start
  293.5 5.8 collective-permute-start
  300.3 5.8 collective-permute-start
  313.8 5.8 collective-permute-start
  320.6 5.8 collective-permute-start
  334.2 5.8 collective-permute-start
  340.9 5.8 collective-permute-start
  352.9 81.0 %reduce-scatter.3.cloned.1.call-done = bf16[8,4096]{1,0:T(8,128)(2,1)} async-done(((bf16[128,4096]{1,0:T(8,128)(2,1)}), bf16[8,4096]{1,0:T(8,128)(2,1)}) %reduce-scatter.3.cloned.1.call-update) | async-done | bytes 65552 | tf_op jit(solution)/shard_map/reduce_scatter | solution.py:104
  435.4 19.1 %all_to_all.10 = bf16[16,2,4096]{2,1,0:T(2,128)(2,1)S(1)} all-to-all(bf16[16,2,4096]{2,1,0:T(2,128)(2,1)S(1)} %reshape.74), channel_id=1, replica_groups=mesh['ctx'=16,'exp'=16] {'exp'}, dimensions={0} | all-to-all | bytes 524288 | tf_op jit(solution)/shard_map/all_to_all | solution.py:134
  455.5 53.0 %all-gather.14.cloned.1.call-done = bf16[512,4096]{1,0:T(8,128)(2,1)} async-done(((bf16[32,4096]{1,0:T(8,128)(2,1)}), bf16[512,4096]{1,0:T(8,128)(2,1)}) %all-gather.14.cloned.1.call-update) | async-done | bytes 4194320 | tf_op jit(solution)/shard_map/all_gather | solution.py:139
  513.9 10.8 %convolution_convert_fusion = bf16[512,4096]{1,0:T(8,128)(2,1)} fusion(bf16[1,448,4096]{2,1,0:T(8,128)(2,1)} %param.32, bf16[512,4096]{1,0:T(8,128)(2,1)} %all-gather.14.cloned.1.call-done, bf16[1,448,4096]{2,1,0:T(8,128)(2,1)} %param.31, f32[512,448]{0,1:T(8,128)S(1)} %fusion.18), kind=kOutput, calls=%fused_computation.19 | convolution fusion | flops 3761569792 | bytes 16646144 | tf_op jit(solution)/shard_map/dot_general | solution.py:147
  524.7 81.0 %reduce-scatter.5.cloned.1.call-done = bf16[32,4096]{1,0:T(8,128)(2,1)} async-done(((bf16[512,4096]{1,0:T(8,128)(2,1)}), bf16[32,4096]{1,0:T(8,128)(2,1)}) %reduce-scatter.5.cloned.1.call-update) | async-done | bytes 262160 | tf_op jit(solution)/shard_map/reduce_scatter | solution.py:148
  607.5 9.3 %all-to-all-start.1 = ((bf16[16,2,4096]{2,1,0:T(2,128)(2,1)}), bf16[16,2,4096]{2,1,0:T(2,128)(2,1)S(1)}, u32[]{:S(2)}, u32[]{:S(2)}) async-start(bf16[16,2,4096]{2,1,0:T(2,128)(2,1)} %reshape.76), calls=%async_computation.3 | async-start | bytes 524288 | tf_op jit(solution)/shard_map/all_to_all | solution.py:151
  617.3 11.2 %all-to-all-done.1 = bf16[16,2,4096]{2,1,0:T(2,128)(2,1)S(1)} async-done(((bf16[16,2,4096]{2,1,0:T(2,128)(2,1)}), bf16[16,2,4096]{2,1,0:T(2,128)(2,1)S(1)}, u32[]{:S(2)}, u32[]{:S(2)}) %all-to-all-start.1) | async-done | bytes 262176 | tf_op jit(solution)/shard_map/all_to_all | solution.py:151
  (121 shorter events, 81.6 us)
Async XLA Ops:
  6.5 44.5 %all-gather.6.cloned.1.call-start = ((), (), s32[]{:S(2)}) async-start(), calls=%async_computation.4 | async-start | bytes 1114112 | tf_op jit(solution)/shard_map/all_gather | solution.py:46
  7.3 101.4 %all-gather.8.cloned.1.call-start = ((), (), s32[]{:S(2)}) async-start(), calls=%async_computation.5 | async-start | bytes 4456448 | tf_op jit(solution)/shard_map/all_gather | solution.py:51
  8.0 159.4 %all-gather.10.cloned.1.call-start = ((), (), s32[]{:S(2)}) async-start(), calls=%async_computation.6 | async-start | bytes 4456448 | tf_op jit(solution)/shard_map/all_gather | solution.py:56
  8.7 339.5 %all-gather.12.cloned.1.call-start = ((), (), s32[]{:S(2)}) async-start(), calls=%async_computation.7 | async-start | bytes 4456448 | tf_op jit(solution)/shard_map/all_gather | solution.py:103
  9.3 424.6 %reduce-scatter.3.cloned.1.call-start = ((), (), s32[]{:S(2)}) async-start(), calls=%async_computation.8 | async-start | bytes 1114112 | tf_op jit(solution)/shard_map/reduce_scatter | solution.py:104
  112.0 58.4 %collective-permute-start.1 = (bf16[3,512]{1,0:T(4,128)(2,1)S(1)}, bf16[3,512]{1,0:T(4,128)(2,1)S(1)}, u32[]{:S(2)}, u32[]{:S(2)}) collective-permute-start(bf16[3,512]{1,0:T(4,128)(2,1)S(1)} %slice.48), channel_id=1, source_target_pairs={{0,16},{16,32},{32,48},{48,64},{64,80},{80,96},{96,112},{112,128},... | collective-permute-start | bytes 9224 | tf_op jit(solution)/shard_map/ppermute | solution.py:18
  257.2 3.7 collective-permute-start
  260.9 4.7 collective-permute-start
  265.5 4.7 collective-permute-start
  270.2 5.1 collective-permute-start
  275.3 4.7 collective-permute-start
  280.0 6.9 %collective-permute-start = (f32[512,16]{0,1:T(8,128)S(1)}, f32[512,16]{0,1:T(8,128)S(1)}, u32[]{:S(2)}, u32[]{:S(2)}) collective-permute-start(f32[512,16]{0,1:T(8,128)S(1)} %multiply_add_fusion.3), channel_id=1, source_target_pairs={{0,16},{16,32},{32,48},{48,64},{64,80},{80,96},{96,112},{112,128},... | collective-permute-start | bytes 98312 | tf_op jit(solution)/shard_map/while/body/eval_jaxpr/ppermute | solution.py:18
  286.8 6.7 %collective-permute-start = (f32[512,16]{0,1:T(8,128)S(1)}, f32[512,16]{0,1:T(8,128)S(1)}, u32[]{:S(2)}, u32[]{:S(2)}) collective-permute-start(f32[512,16]{0,1:T(8,128)S(1)} %multiply_add_fusion.3), channel_id=1, source_target_pairs={{0,16},{16,32},{32,48},{48,64},{64,80},{80,96},{96,112},{112,128},... | collective-permute-start | bytes 98312 | tf_op jit(solution)/shard_map/while/body/eval_jaxpr/ppermute | solution.py:18
  293.5 6.8 %collective-permute-start = (f32[512,16]{0,1:T(8,128)S(1)}, f32[512,16]{0,1:T(8,128)S(1)}, u32[]{:S(2)}, u32[]{:S(2)}) collective-permute-start(f32[512,16]{0,1:T(8,128)S(1)} %multiply_add_fusion.3), channel_id=1, source_target_pairs={{0,16},{16,32},{32,48},{48,64},{64,80},{80,96},{96,112},{112,128},... | collective-permute-start | bytes 98312 | tf_op jit(solution)/shard_map/while/body/eval_jaxpr/ppermute | solution.py:18
  300.3 6.8 %collective-permute-start = (f32[512,16]{0,1:T(8,128)S(1)}, f32[512,16]{0,1:T(8,128)S(1)}, u32[]{:S(2)}, u32[]{:S(2)}) collective-permute-start(f32[512,16]{0,1:T(8,128)S(1)} %multiply_add_fusion.3), channel_id=1, source_target_pairs={{0,16},{16,32},{32,48},{48,64},{64,80},{80,96},{96,112},{112,128},... | collective-permute-start | bytes 98312 | tf_op jit(solution)/shard_map/while/body/eval_jaxpr/ppermute | solution.py:18
  307.1 6.8 %collective-permute-start = (f32[512,16]{0,1:T(8,128)S(1)}, f32[512,16]{0,1:T(8,128)S(1)}, u32[]{:S(2)}, u32[]{:S(2)}) collective-permute-start(f32[512,16]{0,1:T(8,128)S(1)} %multiply_add_fusion.3), channel_id=1, source_target_pairs={{0,16},{16,32},{32,48},{48,64},{64,80},{80,96},{96,112},{112,128},... | collective-permute-start | bytes 98312 | tf_op jit(solution)/shard_map/while/body/eval_jaxpr/ppermute | solution.py:18
  313.8 6.8 %collective-permute-start = (f32[512,16]{0,1:T(8,128)S(1)}, f32[512,16]{0,1:T(8,128)S(1)}, u32[]{:S(2)}, u32[]{:S(2)}) collective-permute-start(f32[512,16]{0,1:T(8,128)S(1)} %multiply_add_fusion.3), channel_id=1, source_target_pairs={{0,16},{16,32},{32,48},{48,64},{64,80},{80,96},{96,112},{112,128},... | collective-permute-start | bytes 98312 | tf_op jit(solution)/shard_map/while/body/eval_jaxpr/ppermute | solution.py:18
  320.6 6.9 %collective-permute-start = (f32[512,16]{0,1:T(8,128)S(1)}, f32[512,16]{0,1:T(8,128)S(1)}, u32[]{:S(2)}, u32[]{:S(2)}) collective-permute-start(f32[512,16]{0,1:T(8,128)S(1)} %multiply_add_fusion.3), channel_id=1, source_target_pairs={{0,16},{16,32},{32,48},{48,64},{64,80},{80,96},{96,112},{112,128},... | collective-permute-start | bytes 98312 | tf_op jit(solution)/shard_map/while/body/eval_jaxpr/ppermute | solution.py:18
  327.6 6.6 %collective-permute-start = (f32[512,16]{0,1:T(8,128)S(1)}, f32[512,16]{0,1:T(8,128)S(1)}, u32[]{:S(2)}, u32[]{:S(2)}) collective-permute-start(f32[512,16]{0,1:T(8,128)S(1)} %multiply_add_fusion.3), channel_id=1, source_target_pairs={{0,16},{16,32},{32,48},{48,64},{64,80},{80,96},{96,112},{112,128},... | collective-permute-start | bytes 98312 | tf_op jit(solution)/shard_map/while/body/eval_jaxpr/ppermute | solution.py:18
  334.2 6.8 %collective-permute-start = (f32[512,16]{0,1:T(8,128)S(1)}, f32[512,16]{0,1:T(8,128)S(1)}, u32[]{:S(2)}, u32[]{:S(2)}) collective-permute-start(f32[512,16]{0,1:T(8,128)S(1)} %multiply_add_fusion.3), channel_id=1, source_target_pairs={{0,16},{16,32},{32,48},{48,64},{64,80},{80,96},{96,112},{112,128},... | collective-permute-start | bytes 98312 | tf_op jit(solution)/shard_map/while/body/eval_jaxpr/ppermute | solution.py:18
  340.9 6.8 %collective-permute-start = (f32[512,16]{0,1:T(8,128)S(1)}, f32[512,16]{0,1:T(8,128)S(1)}, u32[]{:S(2)}, u32[]{:S(2)}) collective-permute-start(f32[512,16]{0,1:T(8,128)S(1)} %multiply_add_fusion.3), channel_id=1, source_target_pairs={{0,16},{16,32},{32,48},{48,64},{64,80},{80,96},{96,112},{112,128},... | collective-permute-start | bytes 98312 | tf_op jit(solution)/shard_map/while/body/eval_jaxpr/ppermute | solution.py:18
  352.1 156.4 %all-gather.14.cloned.1.call-start = ((), (), s32[]{:S(2)}) async-start(), calls=%async_computation.9 | async-start | bytes 4456448 | tf_op jit(solution)/shard_map/all_gather | solution.py:139
  455.3 150.4 %reduce-scatter.5.cloned.1.call-start = ((), (), s32[]{:S(2)}) async-start(), calls=%async_computation.10 | async-start | bytes 4456448 | tf_op jit(solution)/shard_map/reduce_scatter | solution.py:148
  607.5 21.1 %all-to-all-start.1 = ((bf16[16,2,4096]{2,1,0:T(2,128)(2,1)}), bf16[16,2,4096]{2,1,0:T(2,128)(2,1)S(1)}, u32[]{:S(2)}, u32[]{:S(2)}) async-start(bf16[16,2,4096]{2,1,0:T(2,128)(2,1)} %reshape.76), calls=%async_computation.3 | async-start | bytes 524288 | tf_op jit(solution)/shard_map/all_to_all | solution.py:151
  (7 other events, 1065.3 us)
Sparse Core Ops, SparseCore 0:
  9.1 41.8 all-gather.5
  53.4 55.2 all-gather.7
  111.1 56.2 all-gather.9
  169.7 61.4 all-gather.11
  352.2 81.6 reduce-scatter.2
  455.4 53.0 all-gather.13
  524.8 80.7 reduce-scatter.4
where the time goes:
time: 637 us; the launch traced here: 636 us
  waiting for transfers between devices  394 us (62%)
  starting transfers between devices  87.9 us (14%)
  matrix products  67.4 us (11%)
  blocking collectives  65.7 us (10%)
  between operations  13.7 us (2%)
    reduce_scatter x1, waiting for transfers between devices, local(): lax.psum_scatter(jnp.dot(blender_result, out_whole, preferred_element_typ...  81 us
    reduce_scatter x1, waiting for transfers between devices, local(): lax.psum_scatter(partial_out.astype(jnp.bfloat16), 'ctx', scatter_dimensi...  81 us
    ppermute x16, starting transfers between devices, shifted(): return lax.ppermute(shard, axis, pairs)  78.2 us
    all_gather x1, waiting for transfers between devices, local(): lax.all_gather(input_weight, 'ctx', axis=0, tiled=True)  57.7 us
    all_gather x1, waiting for transfers between devices, local(): shard_rows = lax.all_gather(arrived, 'ctx', axis=0, tiled=True)  53 us
    all_gather x1, waiting for transfers between devices, local(): lax.all_gather(gate_weight, 'ctx', axis=0, tiled=True)  52.4 us
    psum x1, blocking collectives, local(): lax.psum(jnp.dot(mixer_in, state_weight, preferred_element_type=jnp.float...  46.7 us
    all_gather x1, waiting for transfers between devices, local(): whole_stretch = lax.all_gather(tokens, 'exp', axis=1, tiled=True)  39.5 us
  transfers between devices with their start and end apart: 24, of which 22 were waited for; matrix products, arithmetic and copies ran while one was open for 8% of the time, Pallas kernels for 0%

commit v1 on v0

--- a/solution.py
+++ b/solution.py
@@ -16,6 +16,12 @@
     devices = lax.axis_size(axis)
     pairs = [(i, i + by) for i in range(devices) if 0 <= i + by < devices]
     return lax.ppermute(shard, axis, pairs)
+
+
+def running_sum(values):
+    length = values.shape[0]
+    lower = jnp.tril(jnp.ones((length, length), jnp.float32))
+    return jnp.dot(lower, values, precision=precise)
 
 
 def causal_part(scores, decay_block, input_block):
@@ -72,7 +78,7 @@
     )
     input_gain = projections[:, :STATE]
     readout = projections[:, STATE:]
-    cumulative = jnp.cumsum(step_size, 0)
+    cumulative = running_sum(step_size)
     scores = jnp.dot(readout, input_gain.T, precision=precise)
     block_width = 128
     block_count = inner_width // block_width
@@ -121,7 +127,11 @@
     selected_entry = jnp.sum(jnp.where(chosen, logits[:, None, :], 0.0), -1)
     shares = jax.nn.sigmoid(selected_entry - selected_entry[:, ::-1])
     flat_hits = chosen.reshape(row_count * TOP, experts).astype(jnp.int32)
-    earlier_hits = jnp.cumsum(flat_hits, 0) - flat_hits
+    earlier_hits = jnp.dot(
+        jnp.tril(jnp.ones((row_count * TOP, row_count * TOP), jnp.float32), -1),
+        flat_hits.astype(jnp.float32),
+        precision=precise,
+    ).astype(jnp.int32)
     slot_index = jnp.sum(earlier_hits * flat_hits, -1)
     target = expert_ids.reshape(-1) * CAP + slot_index
     placed = target[:, None] == jnp.arange(experts * CAP, dtype=jnp.int32)[None, :]

time: 637 us -> 637 us (level)
  no operation moved by 1% of the time
where the time goes in v1:
time: 637 us; the launch traced here: 636 us
  waiting for transfers between devices  394 us (62%)
  starting transfers between devices  87.9 us (14%)
  matrix products  68.1 us (11%)
  blocking collectives  65.7 us (10%)
  between operations  13.7 us (2%)
    reduce_scatter x1, waiting for transfers between devices, local(): lax.psum_scatter(jnp.dot(blender_result, out_whole, preferred_element_typ...  81.1 us
    reduce_scatter x1, waiting for transfers between devices, local(): lax.psum_scatter(partial_out.astype(jnp.bfloat16), 'ctx', scatter_dimensi...  80.9 us
    ppermute x16, starting transfers between devices, shifted(): return lax.ppermute(shard, axis, pairs)  78.2 us
    all_gather x1, waiting for transfers between devices, local(): lax.all_gather(input_weight, 'ctx', axis=0, tiled=True)  57.7 us
    all_gather x1, waiting for transfers between devices, local(): shard_rows = lax.all_gather(arrived, 'ctx', axis=0, tiled=True)  53 us
    all_gather x1, waiting for transfers between devices, local(): lax.all_gather(gate_weight, 'ctx', axis=0, tiled=True)  52.4 us
    psum x1, blocking collectives, local(): lax.psum(jnp.dot(mixer_in, state_weight, preferred_element_type=jnp.float...  46.7 us
    all_gather x1, waiting for transfers between devices, local(): whole_stretch = lax.all_gather(tokens, 'exp', axis=1, tiled=True)  40.3 us
  transfers between devices with their start and end apart: 24, of which 22 were waited for; matrix products, arithmetic and copies ran while one was open for 8% of the time, Pallas kernels for 0%

profile of v1, /device:TPU:1, one launch (start us, length us, event | category | flops | bytes accessed | tf_op | source)
XLA Modules:
  0.0 636.4 jit_solution(114218375562185634)
XLA Ops:
  10.6 40.3 %all-gather.6.cloned.1.call-done = bf16[128,4096]{1,0:T(8,128)(2,1)} async-done(((bf16[128,256]{1,0:T(8,128)(2,1)}), bf16[128,4096]{1,0:T(8,128)(2,1)}) %all-gather.6.cloned.1.call-update) | async-done | bytes 1048592 | tf_op jit(solution)/shard_map/all_gather | solution.py:52
  51.0 57.7 %all-gather.8.cloned.1.call-done = bf16[4096,512]{1,0:T(8,128)(2,1)} async-done(((bf16[256,512]{1,0:T(8,128)(2,1)}), bf16[4096,512]{1,0:T(8,128)(2,1)}) %all-gather.8.cloned.1.call-update) | async-done | bytes 4194320 | tf_op jit(solution)/shard_map/all_gather | solution.py:57
  115.1 52.4 %all-gather.10.cloned.1.call-done = bf16[4096,512]{1,0:T(8,128)(2,1)} async-done(((bf16[256,512]{1,0:T(8,128)(2,1)}), bf16[4096,512]{1,0:T(8,128)(2,1)}) %all-gather.10.cloned.1.call-update) | async-done | bytes 4194320 | tf_op jit(solution)/shard_map/all_gather | solution.py:62
  170.7 46.7 %psum.7 = f32[128,32]{0,1:T(8,128)S(1)} all-reduce(f32[128,32]{0,1:T(8,128)S(1)} %fusion.70), channel_id=1, replica_groups=mesh['ctx'=16,'exp'=16] {'exp'}, use_global_device_ids=true, to_apply=%region_0.1 | all-reduce | flops 4096 | bytes 32768 | tf_op jit(solution)/shard_map/psum | solution.py:76
  218.1 39.1 %while.20 = (s32[]{:T(128)}, f32[4,128,128]{2,1,0:T(8,128)S(1)}, f32[4,128,128]{2,1,0:T(8,128)S(1)}, f32[4,128,128]{2,1,0:T(8,128)S(1)}, f32[128,128]{1,0:T(8,128)S(1)}, /*index=5*/s32[]{:T(128)}) while((s32[]{:T(128)}, f32[4,128,128]{2,1,0:T(8,128)S(1)}, f32[4,128,128]{2,1,0:T(8,128)S(1)}, f32[4,128,128]{2,1,0:T(8,128)S(1)}, ...), condition=%wide.region_2.3_spmd, body=%wide.region_1.2_spmd.sunk | while | flops 35667968 | bytes 688205 | solution.py:87
  218.1 9.7 %fusion.104 = f32[128,1,128]{2,1,0:T(1,128)S(1)} fusion(f32[128,128,1]{1,2,0:T(1,128)S(1)} %bitcast.89, f32[128,128]{1,0:T(8,128)S(1)} %get-tuple-element.140, f32[128,128]{1,0:T(8,128)S(1)} %get-tuple-element.141, pred[128,128]{1,0:T(8,128)(4,1)S(1)} %iota_compare_fusion.10), kind=kOutput, calls=%fused_computation.clone.1 | convolution fusion | flops 35651584 | bytes 278528 | tf_op jit(solution)/shard_map/while/body/eval_jaxpr/ts,tsc,sc->tc/dot_general | solution.py:32
  227.9 9.7 %fusion.104 = f32[128,1,128]{2,1,0:T(1,128)S(1)} fusion(f32[128,128,1]{1,2,0:T(1,128)S(1)} %bitcast.89, f32[128,128]{1,0:T(8,128)S(1)} %get-tuple-element.140, f32[128,128]{1,0:T(8,128)S(1)} %get-tuple-element.141, pred[128,128]{1,0:T(8,128)(4,1)S(1)} %iota_compare_fusion.10), kind=kOutput, calls=%fused_computation.clone.1 | convolution fusion | flops 35651584 | bytes 278528 | tf_op jit(solution)/shard_map/while/body/eval_jaxpr/ts,tsc,sc->tc/dot_general | solution.py:32
  237.6 9.7 %fusion.104 = f32[128,1,128]{2,1,0:T(1,128)S(1)} fusion(f32[128,128,1]{1,2,0:T(1,128)S(1)} %bitcast.89, f32[128,128]{1,0:T(8,128)S(1)} %get-tuple-element.140, f32[128,128]{1,0:T(8,128)S(1)} %get-tuple-element.141, pred[128,128]{1,0:T(8,128)(4,1)S(1)} %iota_compare_fusion.10), kind=kOutput, calls=%fused_computation.clone.1 | convolution fusion | flops 35651584 | bytes 278528 | tf_op jit(solution)/shard_map/while/body/eval_jaxpr/ts,tsc,sc->tc/dot_general | solution.py:32
  247.4 9.7 %fusion.104 = f32[128,1,128]{2,1,0:T(1,128)S(1)} fusion(f32[128,128,1]{1,2,0:T(1,128)S(1)} %bitcast.89, f32[128,128]{1,0:T(8,128)S(1)} %get-tuple-element.140, f32[128,128]{1,0:T(8,128)S(1)} %get-tuple-element.141, pred[128,128]{1,0:T(8,128)(4,1)S(1)} %iota_compare_fusion.10), kind=kOutput, calls=%fused_computation.clone.1 | convolution fusion | flops 35651584 | bytes 278528 | tf_op jit(solution)/shard_map/while/body/eval_jaxpr/ts,tsc,sc->tc/dot_general | solution.py:32
  257.1 90.6 %while.21 = (s32[]{:T(128)}, f32[512,16]{0,1:T(8,128)S(1)}, f32[512]{0:T(512)S(1)}, f32[512,16]{0,1:T(8,128)S(1)}, s32[]{:T(128)}) while((s32[]{:T(128)}, f32[512,16]{0,1:T(8,128)S(1)}, f32[512]{0:T(512)S(1)}, f32[512,16]{0,1:T(8,128)S(1)}, s32[]{:T(128)}) %tuple.40), condition=%wide.region_4.5_spmd, body=%wide.region_3.4_spmd.sunk | while | flops 16386 | bytes 231525 | solution.py:100
  280.0 5.8 collective-permute-start
  293.5 5.8 collective-permute-start
  300.3 5.8 collective-permute-start
  307.1 5.8 collective-permute-start
  313.8 5.8 collective-permute-start
  320.6 5.8 collective-permute-start
  340.9 5.8 collective-permute-start
  352.9 81.1 %reduce-scatter.3.cloned.1.call-done = bf16[8,4096]{1,0:T(8,128)(2,1)} async-done(((bf16[128,4096]{1,0:T(8,128)(2,1)}), bf16[8,4096]{1,0:T(8,128)(2,1)}) %reduce-scatter.3.cloned.1.call-update) | async-done | bytes 65552 | tf_op jit(solution)/shard_map/reduce_scatter | solution.py:110
  435.4 19.1 %all_to_all.10 = bf16[16,2,4096]{2,1,0:T(2,128)(2,1)S(1)} all-to-all(bf16[16,2,4096]{2,1,0:T(2,128)(2,1)S(1)} %reshape.74), channel_id=1, replica_groups=mesh['ctx'=16,'exp'=16] {'exp'}, dimensions={0} | all-to-all | bytes 524288 | tf_op jit(solution)/shard_map/all_to_all | solution.py:144
  455.6 53.0 %all-gather.14.cloned.1.call-done = bf16[512,4096]{1,0:T(8,128)(2,1)} async-done(((bf16[32,4096]{1,0:T(8,128)(2,1)}), bf16[512,4096]{1,0:T(8,128)(2,1)}) %all-gather.14.cloned.1.call-update) | async-done | bytes 4194320 | tf_op jit(solution)/shard_map/all_gather | solution.py:149
  514.0 10.8 %convolution_convert_fusion = bf16[512,4096]{1,0:T(8,128)(2,1)} fusion(bf16[1,448,4096]{2,1,0:T(8,128)(2,1)} %param.32, bf16[512,4096]{1,0:T(8,128)(2,1)} %all-gather.14.cloned.1.call-done, bf16[1,448,4096]{2,1,0:T(8,128)(2,1)} %param.31, f32[512,448]{0,1:T(8,128)S(1)} %fusion.18), kind=kOutput, calls=%fused_computation.19 | convolution fusion | flops 3761569792 | bytes 16646144 | tf_op jit(solution)/shard_map/dot_general | solution.py:157
  524.8 80.9 %reduce-scatter.5.cloned.1.call-done = bf16[32,4096]{1,0:T(8,128)(2,1)} async-done(((bf16[512,4096]{1,0:T(8,128)(2,1)}), bf16[32,4096]{1,0:T(8,128)(2,1)}) %reduce-scatter.5.cloned.1.call-update) | async-done | bytes 262160 | tf_op jit(solution)/shard_map/reduce_scatter | solution.py:158
  607.5 9.4 %all-to-all-start.1 = ((bf16[16,2,4096]{2,1,0:T(2,128)(2,1)}), bf16[16,2,4096]{2,1,0:T(2,128)(2,1)S(1)}, u32[]{:S(2)}, u32[]{:S(2)}) async-start(bf16[16,2,4096]{2,1,0:T(2,128)(2,1)} %reshape.76), calls=%async_computation.3 | async-start | bytes 524288 | tf_op jit(solution)/shard_map/all_to_all | solution.py:161
  617.4 11.2 %all-to-all-done.1 = bf16[16,2,4096]{2,1,0:T(2,128)(2,1)S(1)} async-done(((bf16[16,2,4096]{2,1,0:T(2,128)(2,1)}), bf16[16,2,4096]{2,1,0:T(2,128)(2,1)S(1)}, u32[]{:S(2)}, u32[]{:S(2)}) %all-to-all-start.1) | async-done | bytes 262176 | tf_op jit(solution)/shard_map/all_to_all | solution.py:161
  (122 shorter events, 80.7 us)
Async XLA Ops:
  6.5 44.5 %all-gather.6.cloned.1.call-start = ((), (), s32[]{:S(2)}) async-start(), calls=%async_computation.4 | async-start | bytes 1114112 | tf_op jit(solution)/shard_map/all_gather | solution.py:52
  7.3 101.4 %all-gather.8.cloned.1.call-start = ((), (), s32[]{:S(2)}) async-start(), calls=%async_computation.5 | async-start | bytes 4456448 | tf_op jit(solution)/shard_map/all_gather | solution.py:57
  8.0 159.4 %all-gather.10.cloned.1.call-start = ((), (), s32[]{:S(2)}) async-start(), calls=%async_computation.6 | async-start | bytes 4456448 | tf_op jit(solution)/shard_map/all_gather | solution.py:62
  8.7 339.5 %all-gather.12.cloned.1.call-start = ((), (), s32[]{:S(2)}) async-start(), calls=%async_computation.7 | async-start | bytes 4456448 | tf_op jit(solution)/shard_map/all_gather | solution.py:109
  9.3 424.6 %reduce-scatter.3.cloned.1.call-start = ((), (), s32[]{:S(2)}) async-start(), calls=%async_computation.8 | async-start | bytes 1114112 | tf_op jit(solution)/shard_map/reduce_scatter | solution.py:110
  112.0 58.4 %collective-permute-start.1 = (bf16[3,512]{1,0:T(4,128)(2,1)S(1)}, bf16[3,512]{1,0:T(4,128)(2,1)S(1)}, u32[]{:S(2)}, u32[]{:S(2)}) collective-permute-start(bf16[3,512]{1,0:T(4,128)(2,1)S(1)} %slice.48), channel_id=1, source_target_pairs={{0,16},{16,32},{32,48},{48,64},{64,80},{80,96},{96,112},{112,128},... | collective-permute-start | bytes 9224 | tf_op jit(solution)/shard_map/ppermute | solution.py:18
  257.2 3.7 collective-permute-start
  260.9 4.7 collective-permute-start
  265.5 4.7 collective-permute-start
  270.2 5.1 collective-permute-start
  275.3 4.7 collective-permute-start
  280.0 6.9 %collective-permute-start = (f32[512,16]{0,1:T(8,128)S(1)}, f32[512,16]{0,1:T(8,128)S(1)}, u32[]{:S(2)}, u32[]{:S(2)}) collective-permute-start(f32[512,16]{0,1:T(8,128)S(1)} %multiply_add_fusion.3), channel_id=1, source_target_pairs={{0,16},{16,32},{32,48},{48,64},{64,80},{80,96},{96,112},{112,128},... | collective-permute-start | bytes 98312 | tf_op jit(solution)/shard_map/while/body/eval_jaxpr/ppermute | solution.py:18
  286.8 6.7 %collective-permute-start = (f32[512,16]{0,1:T(8,128)S(1)}, f32[512,16]{0,1:T(8,128)S(1)}, u32[]{:S(2)}, u32[]{:S(2)}) collective-permute-start(f32[512,16]{0,1:T(8,128)S(1)} %multiply_add_fusion.3), channel_id=1, source_target_pairs={{0,16},{16,32},{32,48},{48,64},{64,80},{80,96},{96,112},{112,128},... | collective-permute-start | bytes 98312 | tf_op jit(solution)/shard_map/while/body/eval_jaxpr/ppermute | solution.py:18
  293.5 6.8 %collective-permute-start = (f32[512,16]{0,1:T(8,128)S(1)}, f32[512,16]{0,1:T(8,128)S(1)}, u32[]{:S(2)}, u32[]{:S(2)}) collective-permute-start(f32[512,16]{0,1:T(8,128)S(1)} %multiply_add_fusion.3), channel_id=1, source_target_pairs={{0,16},{16,32},{32,48},{48,64},{64,80},{80,96},{96,112},{112,128},... | collective-permute-start | bytes 98312 | tf_op jit(solution)/shard_map/while/body/eval_jaxpr/ppermute | solution.py:18
  300.3 6.8 %collective-permute-start = (f32[512,16]{0,1:T(8,128)S(1)}, f32[512,16]{0,1:T(8,128)S(1)}, u32[]{:S(2)}, u32[]{:S(2)}) collective-permute-start(f32[512,16]{0,1:T(8,128)S(1)} %multiply_add_fusion.3), channel_id=1, source_target_pairs={{0,16},{16,32},{32,48},{48,64},{64,80},{80,96},{96,112},{112,128},... | collective-permute-start | bytes 98312 | tf_op jit(solution)/shard_map/while/body/eval_jaxpr/ppermute | solution.py:18
  307.1 6.8 %collective-permute-start = (f32[512,16]{0,1:T(8,128)S(1)}, f32[512,16]{0,1:T(8,128)S(1)}, u32[]{:S(2)}, u32[]{:S(2)}) collective-permute-start(f32[512,16]{0,1:T(8,128)S(1)} %multiply_add_fusion.3), channel_id=1, source_target_pairs={{0,16},{16,32},{32,48},{48,64},{64,80},{80,96},{96,112},{112,128},... | collective-permute-start | bytes 98312 | tf_op jit(solution)/shard_map/while/body/eval_jaxpr/ppermute | solution.py:18
  313.8 6.8 %collective-permute-start = (f32[512,16]{0,1:T(8,128)S(1)}, f32[512,16]{0,1:T(8,128)S(1)}, u32[]{:S(2)}, u32[]{:S(2)}) collective-permute-start(f32[512,16]{0,1:T(8,128)S(1)} %multiply_add_fusion.3), channel_id=1, source_target_pairs={{0,16},{16,32},{32,48},{48,64},{64,80},{80,96},{96,112},{112,128},... | collective-permute-start | bytes 98312 | tf_op jit(solution)/shard_map/while/body/eval_jaxpr/ppermute | solution.py:18
  320.6 6.9 %collective-permute-start = (f32[512,16]{0,1:T(8,128)S(1)}, f32[512,16]{0,1:T(8,128)S(1)}, u32[]{:S(2)}, u32[]{:S(2)}) collective-permute-start(f32[512,16]{0,1:T(8,128)S(1)} %multiply_add_fusion.3), channel_id=1, source_target_pairs={{0,16},{16,32},{32,48},{48,64},{64,80},{80,96},{96,112},{112,128},... | collective-permute-start | bytes 98312 | tf_op jit(solution)/shard_map/while/body/eval_jaxpr/ppermute | solution.py:18
  327.6 6.6 %collective-permute-start = (f32[512,16]{0,1:T(8,128)S(1)}, f32[512,16]{0,1:T(8,128)S(1)}, u32[]{:S(2)}, u32[]{:S(2)}) collective-permute-start(f32[512,16]{0,1:T(8,128)S(1)} %multiply_add_fusion.3), channel_id=1, source_target_pairs={{0,16},{16,32},{32,48},{48,64},{64,80},{80,96},{96,112},{112,128},... | collective-permute-start | bytes 98312 | tf_op jit(solution)/shard_map/while/body/eval_jaxpr/ppermute | solution.py:18
  334.2 6.8 %collective-permute-start = (f32[512,16]{0,1:T(8,128)S(1)}, f32[512,16]{0,1:T(8,128)S(1)}, u32[]{:S(2)}, u32[]{:S(2)}) collective-permute-start(f32[512,16]{0,1:T(8,128)S(1)} %multiply_add_fusion.3), channel_id=1, source_target_pairs={{0,16},{16,32},{32,48},{48,64},{64,80},{80,96},{96,112},{112,128},... | collective-permute-start | bytes 98312 | tf_op jit(solution)/shard_map/while/body/eval_jaxpr/ppermute | solution.py:18
  340.9 6.8 %collective-permute-start = (f32[512,16]{0,1:T(8,128)S(1)}, f32[512,16]{0,1:T(8,128)S(1)}, u32[]{:S(2)}, u32[]{:S(2)}) collective-permute-start(f32[512,16]{0,1:T(8,128)S(1)} %multiply_add_fusion.3), channel_id=1, source_target_pairs={{0,16},{16,32},{32,48},{48,64},{64,80},{80,96},{96,112},{112,128},... | collective-permute-start | bytes 98312 | tf_op jit(solution)/shard_map/while/body/eval_jaxpr/ppermute | solution.py:18
  352.1 156.4 %all-gather.14.cloned.1.call-start = ((), (), s32[]{:S(2)}) async-start(), calls=%async_computation.9 | async-start | bytes 4456448 | tf_op jit(solution)/shard_map/all_gather | solution.py:149
  455.3 150.3 %reduce-scatter.5.cloned.1.call-start = ((), (), s32[]{:S(2)}) async-start(), calls=%async_computation.10 | async-start | bytes 4456448 | tf_op jit(solution)/shard_map/reduce_scatter | solution.py:158
  607.5 21.1 %all-to-all-start.1 = ((bf16[16,2,4096]{2,1,0:T(2,128)(2,1)}), bf16[16,2,4096]{2,1,0:T(2,128)(2,1)S(1)}, u32[]{:S(2)}, u32[]{:S(2)}) async-start(bf16[16,2,4096]{2,1,0:T(2,128)(2,1)} %reshape.76), calls=%async_computation.3 | async-start | bytes 524288 | tf_op jit(solution)/shard_map/all_to_all | solution.py:161
  (8 other events, 550.8 us)
Sparse Core Ops, SparseCore 0:
  9.1 41.8 all-gather.5
  53.4 55.2 all-gather.7
  111.1 56.2 all-gather.9
  169.7 61.4 all-gather.11
  352.3 81.6 reduce-scatter.2
  455.4 53.0 all-gather.13
  524.9 80.7 reduce-scatter.4

commit v2 on v0

v2 whole, which is shorter than its diff:
```python
import functools

import jax
import jax.numpy as jnp
from jax import lax
from jax.experimental import pallas as pl
from jax.experimental.pallas import tpu as pltpu
from jax.sharding import PartitionSpec as P

STATE = 16
CONV = 4
TOP = 2
CAP = 2
SIDE = 4
PLANE = SIDE * SIDE
DEPTH = 8
EXPS = 2 * DEPTH
CHUNK = 8

precise = lax.Precision.HIGHEST
f32 = jnp.float32
bf16 = jnp.bfloat16
MESH = pl.DeviceIdType.MESH


def remote(src, dst, send_sem, recv_sem, device):
    return pltpu.make_async_remote_copy(
        src_ref=src,
        dst_ref=dst,
        send_sem=send_sem,
        recv_sem=recv_sem,
        device_id=device,
        device_id_type=MESH,
    )


def greet(ctx_peers, exp_peers):
    c, e = lax.axis_index("ctx"), lax.axis_index("exp")
    barrier = pltpu.get_barrier_semaphore()
    count = 0
    if ctx_peers:

        @pl.loop(1, PLANE)
        def _(d):
            pl.semaphore_signal(
                barrier, inc=1, device_id=(lax.rem(c + d, PLANE), e), device_id_type=MESH
            )

        count += PLANE - 1
    if exp_peers:

        @pl.loop(1, EXPS)
        def _(d):
            pl.semaphore_signal(
                barrier, inc=1, device_id=(c, lax.rem(e + d, EXPS)), device_id_type=MESH
            )

        count += EXPS - 1
    pl.semaphore_wait(barrier, count)


class PlaneView:
    def __init__(self, x_first):
        c, self.e = lax.axis_index("ctx"), lax.axis_index("exp")
        y, x = c // SIDE, lax.rem(c, SIDE)
        self.x_first = x_first
        self.f, self.s = (x, y) if x_first else (y, x)

    def at(self, df, ds):
        f, s = lax.rem(self.f + df + SIDE, SIDE), lax.rem(self.s + ds + SIDE, SIDE)
        return s * SIDE + f if self.x_first else f * SIDE + s


class PlaneGather:
    ORDER = (0, -1, 1, 2)

    def __init__(self, part, x_first, send, recv):
        self.view, self.part, self.send, self.recv = PlaneView(x_first), part, send, recv

    def copy(self, k, slot, which, target):
        block = self.part(slot, which)
        return remote(block, block, self.send.at[k], self.recv.at[k], (target, self.view.e))

    def sent(self, k):
        at = self.view.at
        if k < 4:
            slot, which = ((0, None), (0, None), (-1, 0), (1, 1))[k]
            return self.copy(k, at(slot, 0), which, at(1 if k % 2 == 0 else -1, 0))
        df, kind = self.ORDER[(k - 4) // 4], (k - 4) % 4
        slot, which = ((0, None), (0, None), (-1, 0), (1, 1))[kind]
        return self.copy(k, at(df, slot), which, at(0, 1 if kind % 2 == 0 else -1))

    def arrived(self, k):
        at = self.view.at
        if k < 4:
            slot, which = ((-1, None), (1, None), (2, 0), (2, 1))[k]
            return self.copy(k, at(slot, 0), which, at(0, 0))
        df, kind = self.ORDER[(k - 4) // 4], (k - 4) % 4
        slot, which = ((-1, None), (1, None), (2, 0), (2, 1))[kind]
        return self.copy(k, at(df, slot), which, at(0, 0))

    def start(self, *ks):
        for k in ks:
            self.sent(k).start()

    def await_(self, *ks):
        for k in ks:
            self.arrived(k).wait_recv()

    def finish(self):
        for k in range(20):
            self.sent(k).wait_send()


def first_sends(gathers):
    for g in gathers:
        g.start(0, 1)
    for g in gathers:
        g.start(4, 5)


def first_hop(gathers):
    for g in gathers:
        g.await_(0)
        g.start(2, 8, 9)
        g.await_(1)
        g.start(3, 12, 13)


def first_axis_done(gathers):
    for g in gathers:
        g.await_(2, 3)
        g.start(16, 17)


def second_hop(gathers):
    for j in range(4):
        for g in gathers:
            g.await_(4 + 4 * j)
            g.start(6 + 4 * j)
            g.await_(5 + 4 * j)
            g.start(7 + 4 * j)


def second_axis_done(gathers):
    for j in range(4):
        for g in gathers:
            g.await_(6 + 4 * j, 7 + 4 * j)


def rows_part(ref, begin, length):
    def part(slot, which):
        if which is None:
            return ref.at[slot, pl.ds(begin, length), :]
        return ref.at[slot, pl.ds(begin + which * (length // 2), length // 2), :]

    return part


def columns_part(ref, begin, length):
    def part(slot, which):
        width = ref.shape[-1]
        if which is None:
            return ref.at[slot, pl.ds(begin, length), :]
        return ref.at[slot, pl.ds(begin, length), pl.ds(which * (width // 2), width // 2)]

    return part


def mixer_kernel(
    tok,
    wx,
    wz,
    cw,
    cb,
    sw,
    ss,
    sg,
    wo,
    out,
    tg,
    gx,
    gz,
    go,
    acc_x,
    acc_z,
    xb,
    halo,
    ext,
    mw,
    keep,
    cum,
    read,
    pj,
    sb,
    st,
    part,
    pair,
    summed,
    landed,
    town,
    wx_send,
    wx_recv,
    wz_send,
    wz_recv,
    wo_send,
    wo_recv,
    tok_send,
    tok_recv,
    core_send,
    core_recv,
    halo_send,
    halo_recv,
    pj_send,
    pj_recv,
    st_send,
    st_recv,
    pair_send,
    pair_recv,
    sum_send,
    sum_recv,
):
    c, e = lax.axis_index("ctx"), lax.axis_index("exp")
    z, core = e // 2, lax.rem(e, 2)
    partner = z * 2 + 1 - core
    rows, inner = acc_x.shape

    gx[c] = wx[...]
    gz[c] = wz[...]
    go[c] = wo[...]
    tg[e] = tok[...]

    greet(True, True)

    weights = (
        PlaneGather(rows_part(gx, 0, gx.shape[1]), True, wx_send, wx_recv),
        PlaneGather(rows_part(gz, 0, gz.shape[1]), False, wz_send, wz_recv),
    )
    half = go.shape[1] // 2
    outs = (
        PlaneGather(rows_part(go, 0, half), True, wo_send.at[0], wo_recv.at[0]),
        PlaneGather(rows_part(go, half, half), False, wo_send.at[1], wo_recv.at[1]),
    )
    first_sends(weights)

    def tok_copy(d, slot):
        target = lax.rem(z + d, DEPTH) * 2 + core
        return remote(tg.at[slot], tg.at[slot], tok_send.at[d], tok_recv.at[d], (c, target))

    def core_copy(d, slot):
        return remote(tg.at[slot], tg.at[slot], core_send.at[d], core_recv.at[d], (c, partner))

    def from_z(d, k):
        return lax.rem(z - d + DEPTH, DEPTH) * 2 + k

    core_copy(0, e).start()

    @pl.loop(1, DEPTH)
    def _(d):
        tok_copy(d, e).start()

    first_hop(weights)

    @pl.loop(1, DEPTH)
    def _(d):
        tok_copy(d, from_z(d, core)).wait_recv()
        core_copy(d, from_z(d, core)).start()

    @pl.loop(0, DEPTH)
    def _(d):
        core_copy(d, from_z(d, 1 - core)).wait_recv()

    acc_x[...] = jnp.zeros_like(acc_x)
    acc_z[...] = jnp.zeros_like(acc_z)

    def multiply(acc, gathered, slot_of):
        @pl.loop(0, SIDE)
        def _(i):
            slot = slot_of(i)
            acc[...] += jnp.dot(tg[slot], gathered[slot], preferred_element_type=f32)

    first_axis_done(weights)
    view_x, view_z = weights[0].view, weights[1].view
    multiply(acc_x, gx, lambda i: view_x.at(i, 0))
    multiply(acc_z, gz, lambda i: view_z.at(i, 0))

    own_rows = out.shape[0]
    picked = lax.broadcasted_iota(jnp.int32, (own_rows, rows), 1) == (
        lax.broadcasted_iota(jnp.int32, (own_rows, rows), 0) + e * own_rows
    )
    picker = picked.astype(f32).astype(bf16)
    width = tg.shape[2]

    @pl.loop(0, EXPS)
    def _(j):
        town[j] = jnp.dot(picker, tg[j], preferred_element_type=f32)

    second_hop(weights)
    for step in (-1, 1):
        multiply(acc_x, gx, lambda i: view_x.at(i, step))
        multiply(acc_z, gz, lambda i: view_z.at(i, step))
    second_axis_done(weights)
    first_sends(outs)
    multiply(acc_x, gx, lambda i: view_x.at(i, 2))
    multiply(acc_z, gz, lambda i: view_z.at(i, 2))

    xb[...] = acc_x[...].astype(bf16)
    held = halo.shape[0]

    def halo_copy():
        return remote(
            xb.at[pl.ds(rows - held, held), :],
            halo,
            halo_send,
            halo_recv,
            (lax.rem(c + 1, PLANE), e),
        )

    @pl.when(c < PLANE - 1)
    def _():
        halo_copy().start()

    ext[pl.ds(held, rows), :] = xb[...].astype(f32)
    keep[...] = jnp.exp(-ss[...])

    @pl.when(c == 0)
    def _():
        halo[...] = jnp.zeros_like(halo)

    @pl.when(c > 0)
    def _():
        halo_copy().wait_recv()

    ext[pl.ds(0, held), :] = halo[...].astype(f32)
    filtered = jnp.broadcast_to(cb[...], (rows, inner))
    for offset in range(CONV):
        begin = held - (CONV - 1) + offset
        filtered = filtered + cw[pl.ds(offset, 1), :] * ext[pl.ds(begin, rows), :]
    mixer_in = (filtered / (1.0 + jnp.exp(-filtered))).astype(bf16)
    mw[...] = mixer_in.astype(f32)

    pj[e] = lax.dot_general(
        sw[...], mixer_in, (((0,), (1,)), ((), ())), preferred_element_type=f32
    )

    def pj_copy(d, slot):
        target = lax.rem(e + d, EXPS)
        return remote(pj.at[slot], pj.at[slot], pj_send.at[d], pj_recv.at[d], (c, target))

    @pl.loop(1, EXPS)
    def _(d):
        pj_copy(d, e).start()

    first_hop(outs)

    @pl.loop(1, EXPS)
    def _(d):
        pj_copy(d, lax.rem(e - d + EXPS, EXPS)).wait_recv()

    projected = pj[0]
    for j in range(1, EXPS):
        projected = projected + pj[j]
    chunks = rows // CHUNK
    for j in range(chunks):
        sb[j, :, pl.ds(0, CHUNK)] = projected[:, j * CHUNK : (j + 1) * CHUNK]

    def advance(j, carry):
        state, decay = carry
        vectors = sb[j]
        first = pl.multiple_of(j * CHUNK, CHUNK)
        keeps, inputs = keep[pl.ds(first, CHUNK), :], mw[pl.ds(first, CHUNK), :]
        for i in range(CHUNK):
            kept = keeps[i : i + 1, :]
            state = kept * state + inputs[i : i + 1, :] * vectors[:STATE, i : i + 1]
            decay = decay * kept
            read[pl.ds(first + i, 1), :] = jnp.sum(
                vectors[STATE:, i : i + 1] * state, axis=0, keepdims=True
            )
            cum[pl.ds(first + i, 1), :] = decay
        return state, decay

    state, decay = lax.fori_loop(
        0, chunks, advance, (jnp.zeros((STATE, inner), f32), jnp.ones((1, inner), f32))
    )

    st[c, pl.ds(0, STATE), :] = state
    st[c, pl.ds(STATE, 8), :] = jnp.broadcast_to(decay, (8, inner))

    def st_copy(d, slot, target):
        return remote(st.at[slot], st.at[slot], st_send.at[d], st_recv.at[d], (target, e))

    @pl.loop(1, PLANE - c)
    def _(d):
        st_copy(d, c, lax.rem(c + d, PLANE)).start()

    first_axis_done(outs)

    def enter(source, entering):
        st_copy(c - source, source, lax.rem(source + 1, PLANE)).wait_recv()
        return st[source, pl.ds(STATE, 1), :] * entering + st[source, pl.ds(0, STATE), :]

    entering = lax.fori_loop(0, c, enter, jnp.zeros((STATE, inner), f32))
    carried = cum[...] * lax.dot_general(
        projected[STATE:, :],
        entering,
        (((0,), (0,)), ((), ())),
        preferred_element_type=f32,
        precision=precise,
    )
    gate = acc_z[...].astype(bf16).astype(f32)
    mixed = (read[...] + carried + sg[...] * mw[...]) * (gate / (1.0 + jnp.exp(-gate)))
    xb_out = mixed.astype(bf16)
    second_hop(outs)
    second_axis_done(outs)

    columns = go.shape[2]

    @pl.loop(0, PLANE)
    def _(j):
        block = jnp.dot(xb_out, go[j], preferred_element_type=f32)
        at = pl.ds(pl.multiple_of(j * columns, columns), columns)
        for i in range(EXPS):
            part[i % 2, i // 2, :, at] = block[i * own_rows : (i + 1) * own_rows].astype(bf16)

    pair_copy = remote(part.at[1 - core], pair, pair_send, pair_recv, (c, partner))
    pair_copy.start()
    pair_copy.wait_recv()

    def sum_copy(d, mine, theirs, target):
        return remote(
            summed.at[mine], landed.at[theirs], sum_send.at[d], sum_recv.at[d], (c, target)
        )

    @pl.loop(1, DEPTH)
    def _(d):
        there = lax.rem(z + d, DEPTH)
        summed[there] = (part[core, there].astype(f32) + pair[there].astype(f32)).astype(bf16)
        sum_copy(d, there, z, there * 2 + core).start()

    for j in range(EXPS):
        out[:, pl.ds(j * width, width)] = town[j].astype(bf16)
    own = part[core, z].astype(f32) + pair[z].astype(f32)

    def collect(d, total):
        source = lax.rem(z - d + DEPTH, DEPTH)
        sum_copy(d, source, source, source * 2 + core).wait_recv()
        return total + landed[source].astype(f32)

    total = lax.fori_loop(1, DEPTH, collect, own)
    out[...] = (out[...].astype(f32) + total).astype(bf16)

    for g in weights + outs:
        g.finish()
    core_copy(0, e).wait_send()

    @pl.loop(1, DEPTH)
    def _(d):
        tok_copy(d, e).wait_send()
        core_copy(d, from_z(d, core)).wait_send()
        there = lax.rem(z + d, DEPTH)
        sum_copy(d, there, z, there * 2 + core).wait_send()

    @pl.when(c < PLANE - 1)
    def _():
        halo_copy().wait_send()

    @pl.loop(1, EXPS)
    def _(d):
        pj_copy(d, e).wait_send()

    @pl.loop(1, PLANE - c)
    def _(d):
        st_copy(d, c, lax.rem(c + d, PLANE)).wait_send()

    pair_copy.wait_send()


def mixer(tokens, wx, wz, cw, cb, sw, ss, sg, wo):
    rows, width = tokens.shape
    inner = wx.shape[1]
    model = width * EXPS
    own = rows // EXPS
    dma = pltpu.SemaphoreType.DMA
    vmem = pl.BlockSpec(memory_space=pltpu.VMEM)
    return pl.pallas_call(
        mixer_kernel,
        out_shape=jax.ShapeDtypeStruct((own, model), bf16),
        in_specs=[vmem] * 9,
        out_specs=vmem,
        scratch_shapes=[
            pltpu.VMEM((EXPS, rows, width), bf16),
            pltpu.VMEM((PLANE, *wx.shape), bf16),
            pltpu.VMEM((PLANE, *wz.shape), bf16),
            pltpu.VMEM((PLANE, *wo.shape), bf16),
            pltpu.VMEM((rows, inner), f32),
            pltpu.VMEM((rows, inner), f32),
            pltpu.VMEM((rows, inner), bf16),
            pltpu.VMEM((16, inner), bf16),
            pltpu.VMEM((rows + 16, inner), f32),
            pltpu.VMEM((rows, inner), f32),
            pltpu.VMEM((rows, inner), f32),
            pltpu.VMEM((rows, inner), f32),
            pltpu.VMEM((rows, inner), f32),
            pltpu.VMEM((EXPS, 2 * STATE, rows), f32),
            pltpu.VMEM((rows // CHUNK, 2 * STATE, 128), f32),
            pltpu.VMEM((PLANE, STATE + 8, inner), f32),
            pltpu.VMEM((2, DEPTH, own, model), bf16),
            pltpu.VMEM((DEPTH, own, model), bf16),
            pltpu.VMEM((DEPTH, own, model), bf16),
            pltpu.VMEM((DEPTH, own, model), bf16),
            pltpu.VMEM((EXPS, own, width), f32),
            dma((20,)),
            dma((20,)),
            dma((20,)),
            dma((20,)),
            dma((2, 20)),
            dma((2, 20)),
            dma((DEPTH,)),
            dma((DEPTH,)),
            dma((DEPTH,)),
            dma((DEPTH,)),
            dma,
            dma,
            dma((EXPS,)),
            dma((EXPS,)),
            dma((PLANE,)),
            dma((PLANE,)),
            dma,
            dma,
            dma((DEPTH,)),
            dma((DEPTH,)),
        ],
        compiler_params=pltpu.CompilerParams(
            collective_id=0, has_side_effects=True, vmem_limit_bytes=48 << 20
        ),
        name="mixer",
    )(tokens, wx, wz, cw, cb.reshape(1, -1), sw, ss, sg.reshape(1, -1), wo)


class PlaneReduce:
    ORDER = (2, -1, 1, 0)

    def __init__(self, part, late, x_first, send, recv):
        self.view, self.part, self.late = PlaneView(x_first), part, late
        self.send, self.recv = send, recv

    def place(self, k, step):
        if k < 16:
            return self.view.at(self.ORDER[k // 4], step)
        return self.view.at(step, 0)

    def copy(self, k):
        kind = k % 4
        step, which, to = ((2, 0, 1), (2, 1, -1), (1, None, 1), (-1, None, -1))[kind]
        target = self.view.at(0, to) if k < 16 else self.view.at(to, 0)
        return remote(
            self.part(self.place(k, step), which),
            self.late(k, which),
            self.send.at[k],
            self.recv.at[k],
            (target, self.view.e),
        )

    def add(self, k, step, which):
        self.copy(k).wait_recv()
        mine = self.part(self.place(k, step), which)
        mine[...] = (mine[...].astype(f32) + self.late(k, which)[...].astype(f32)).astype(bf16)

    def far(self, j):
        self.copy(4 * j).start()
        self.copy(4 * j + 1).start()

    def near(self, j):
        self.add(4 * j, 1, 0)
        self.copy(4 * j + 2).start()
        self.add(4 * j + 1, -1, 1)
        self.copy(4 * j + 3).start()

    def close(self, j):
        self.add(4 * j + 2, 0, None)
        self.add(4 * j + 3, 0, None)

    def finish(self):
        for k in range(20):
            self.copy(k).wait_send()


def expert_kernel(
    arrived,
    wg_hbm,
    wu_hbm,
    wd_hbm,
    out,
    wg,
    wu,
    wd,
    rows_in,
    acc_g,
    acc_u,
    sums,
    late,
    load_sem,
    ag_send,
    ag_recv,
    rs_send,
    rs_recv,
):
    c = lax.axis_index("ctx")
    loads = [
        pltpu.make_async_copy(src, dst, load_sem.at[i])
        for i, (src, dst) in enumerate(((wg_hbm, wg), (wu_hbm, wu), (wd_hbm, wd)))
    ]
    for load in loads:
        load.start()
    rows_in[c] = arrived[...]
    greet(True, False)
    slots, model = arrived.shape
    half = slots // 2
    gathers = (
        PlaneGather(columns_part(rows_in, 0, half), True, ag_send.at[0], ag_recv.at[0]),
        PlaneGather(columns_part(rows_in, half, half), False, ag_send.at[1], ag_recv.at[1]),
    )
    first_sends(gathers)
    first_hop(gathers)
    first_axis_done(gathers)
    second_hop(gathers)
    second_axis_done(gathers)
    for load in loads:
        load.wait()

    units = wg.shape[0]
    many = PLANE * slots
    step = 512
    acc_g[...] = jnp.zeros_like(acc_g)
    acc_u[...] = jnp.zeros_like(acc_u)

    @pl.loop(0, model // step)
    def _(k):
        at = pl.ds(pl.multiple_of(k * step, step), step)
        block = rows_in[:, :, at].reshape(many, step)
        turned = (((1,), (1,)), ((), ()))
        acc_g[...] += lax.dot_general(block, wg[:, at], turned, preferred_element_type=f32)
        acc_u[...] += lax.dot_general(block, wu[:, at], turned, preferred_element_type=f32)

    gate = acc_g[...]
    hidden = ((gate / (1.0 + jnp.exp(-gate))) * acc_u[...]).astype(bf16)

    @pl.loop(0, model // step)
    def _(k):
        at = pl.ds(pl.multiple_of(k * step, step), step)
        block = jnp.dot(hidden, wd[:, at], preferred_element_type=f32)
        sums[:, :, at] = block.astype(bf16).reshape(PLANE, slots, step)

    def landing(i):
        def at(k, which):
            if which is None:
                return late.at[i, k]
            return late.at[i, k, :, pl.ds(which * (model // 2), model // 2)]

        return at

    reduces = (
        PlaneReduce(columns_part(sums, 0, half), landing(0), True, rs_send.at[0], rs_recv.at[0]),
        PlaneReduce(columns_part(sums, half, half), landing(1), False, rs_send.at[1], rs_recv.at[1]),
    )
    for j in range(4):
        for r in reduces:
            r.far(j)
    for j in range(4):
        for r in reduces:
            r.near(j)
    for j in range(4):
        for r in reduces:
            r.close(j)
            if j == 0:
                r.far(4)
    for r in reduces:
        r.near(4)
    for r in reduces:
        r.close(4)
    out[...] = sums[c]
    for g in gathers:
        g.finish()
    for r in reduces:
        r.finish()


def experts_of(arrived, wg, wu, wd):
    slots, model = arrived.shape
    units = wg.shape[0]
    dma = pltpu.SemaphoreType.DMA
    vmem = pl.BlockSpec(memory_space=pltpu.VMEM)
    anywhere = pl.BlockSpec(memory_space=pl.ANY)
    return pl.pallas_call(
        expert_kernel,
        out_shape=jax.ShapeDtypeStruct((slots, model), bf16),
        in_specs=[vmem, anywhere, anywhere, anywhere],
        out_specs=vmem,
        scratch_shapes=[
            pltpu.VMEM((units, model), bf16),
            pltpu.VMEM((units, model), bf16),
            pltpu.VMEM((units, model), bf16),
            pltpu.VMEM((PLANE, slots, model), bf16),
            pltpu.VMEM((PLANE * slots, units), f32),
            pltpu.VMEM((PLANE * slots, units), f32),
            pltpu.VMEM((PLANE, slots, model), bf16),
            pltpu.VMEM((2, 20, slots // 2, model), bf16),
            dma((3,)),
            dma((2, 20)),
            dma((2, 20)),
            dma((2, 20)),
            dma((2, 20)),
        ],
        compiler_params=pltpu.CompilerParams(
            collective_id=1, has_side_effects=True, vmem_limit_bytes=56 << 20
        ),
        name="experts",
    )(arrived, wg, wu, wd)


def exchange_kernel(given, taken, own_sem, send, recv):
    c, e = lax.axis_index("ctx"), lax.axis_index("exp")
    own = pltpu.make_async_copy(given.at[e], taken.at[e], own_sem)
    own.start()
    greet(False, True)

    def copy(d, mine, theirs, target):
        return remote(given.at[mine], taken.at[theirs], send.at[d], recv.at[d], (c, target))

    @pl.loop(1, EXPS)
    def _(d):
        there = lax.rem(e + d, EXPS)
        copy(d, there, e, there).start()

    own.wait()

    @pl.loop(1, EXPS)
    def _(d):
        source = lax.rem(e - d + EXPS, EXPS)
        copy(d, source, source, source).wait_recv()

    @pl.loop(1, EXPS)
    def _(d):
        there = lax.rem(e + d, EXPS)
        copy(d, there, e, there).wait_send()


def exchange(blocks, collective_id):
    dma = pltpu.SemaphoreType.DMA
    vmem = pl.BlockSpec(memory_space=pltpu.VMEM)
    return pl.pallas_call(
        exchange_kernel,
        out_shape=jax.ShapeDtypeStruct(blocks.shape, blocks.dtype),
        in_specs=[vmem],
        out_specs=vmem,
        scratch_shapes=[dma, dma((EXPS,)), dma((EXPS,))],
        compiler_params=pltpu.CompilerParams(collective_id=collective_id, has_side_effects=True),
        name=f"exchange_{collective_id}",
    )(blocks)


def local(
    tokens,
    input_weight,
    gate_weight,
    conv_weight,
    conv_bias,
    state_weight,
    step_size,
    skip_gain,
    output_weight,
    norm_gain,
    router_weight,
    expert_gate,
    expert_up,
    expert_down,
    expert_ids,
):
    residual = mixer(
        tokens,
        input_weight,
        gate_weight,
        conv_weight,
        conv_bias,
        state_weight,
        step_size,
        skip_gain,
        output_weight,
    )
    row_count = expert_ids.shape[0]
    stream = residual.astype(f32)
    normed = (
        stream
        * lax.rsqrt(jnp.mean(stream * stream, -1, keepdims=True) + 1e-05)
        * norm_gain[None, :]
    ).astype(bf16)
    logits = jnp.dot(normed, router_weight, preferred_element_type=f32)
    experts = router_weight.shape[1]
    expert_range = jnp.arange(experts, dtype=jnp.int32)
    chosen = expert_ids[:, :, None] == expert_range[None, None, :]
    selected_entry = jnp.sum(jnp.where(chosen, logits[:, None, :], 0.0), -1)
    shares = jax.nn.sigmoid(selected_entry - selected_entry[:, ::-1])
    flat_hits = chosen.reshape(row_count * TOP, experts).astype(f32)
    earlier_hits = jnp.dot(
        jnp.tril(jnp.ones((row_count * TOP, row_count * TOP), f32), -1),
        flat_hits,
        precision=precise,
    )
    slot_index = jnp.sum(earlier_hits * flat_hits, -1).astype(jnp.int32)
    target = expert_ids.reshape(-1) * CAP + slot_index
    placed = target[:, None] == jnp.arange(experts * CAP, dtype=jnp.int32)[None, :]
    placed = placed.reshape(row_count, TOP, experts * CAP)
    selector = jnp.any(placed, 1).astype(bf16)
    outgoing = lax.dot_general(
        selector, normed, (((0,), (0,)), ((), ())), preferred_element_type=f32
    ).astype(bf16)
    outgoing = outgoing.reshape(experts, CAP, -1)
    arrived = exchange(outgoing, 2).reshape(experts * CAP, -1)
    finished = experts_of(arrived, expert_gate[0], expert_up[0], expert_down[0])
    returned = exchange(finished.reshape(experts, CAP, -1), 3)
    returned = returned.reshape(experts * CAP, -1).astype(f32)
    combine = jnp.sum(jnp.where(placed, shares[:, :, None], 0.0), 1)
    moe_out = jnp.dot(combine, returned, precision=precise)
    return (stream + moe_out).astype(bf16)


def solution(mesh):
    in_specs = (
        P("ctx", "exp"),
        P("ctx", "exp"),
        P("ctx", "exp"),
        P(None, "exp"),
        P("exp"),
        P("exp", None),
        P("ctx", "exp"),
        P("exp"),
        P("exp", "ctx"),
        P(),
        P(),
        P("exp", "ctx", None),
        P("exp", "ctx", None),
        P("exp", "ctx", None),
        P(("ctx", "exp"), None),
    )
    out_specs = P(("ctx", "exp"), None)
    return jax.shard_map(local, mesh=mesh, in_specs=in_specs, out_specs=out_specs, check_vma=False)
```

time: 637 us -> 229 us (0.36)
  waiting for transfers between devices: 394 us -> 0 us
  Pallas kernels: 0 us -> 210 us
  starting transfers between devices: 87.9 us -> 0 us
  blocking collectives: 65.7 us -> 0 us
  matrix products: 67.4 us -> 2.93 us
  between operations: 13.7 us -> 0.09 us
  local copies, waits for them, and re-layouts: 4.31 us -> 14.2 us
    pallas_call x0 -> x4, Pallas kernels: none -> 210 us  [the longest x1 115 us: mixer(): pl.pallas_call(mixer_kernel, out_shape=jax.ShapeDtypeStruct((own, model),...]
    all_gather x5 -> x0, waiting for transfers between devices: 203 us -> none  [the longest x1 57.7 us: local(): lax.all_gather(input_weight, 'ctx', axis=0, tiled=True)]
    reduce_scatter x2 -> x0, waiting for transfers between devices: 162 us -> none  [the longest x1 81 us: local(): lax.psum_scatter(jnp.dot(blender_result, out_whole, preferred_element_typ...]
    ppermute x16 -> x0, starting transfers between devices: 78.2 us -> none  [shifted(): return lax.ppermute(shard, axis, pairs)]
    dot_general x14 -> x2, matrix products: 66.3 us -> 1.07 us  [the longest x1 0.93 us: local(): logits = jnp.dot(normed, router_weight, preferred_element_type=f32)]
    psum x1 -> x0, blocking collectives: 46.7 us -> none  [local(): lax.psum(jnp.dot(mixer_in, state_weight, preferred_element_type=jnp.float...]
    all_to_all x1 -> x0, blocking collectives: 19.1 us -> none  [local(): lax.all_to_all(outgoing, 'exp', split_axis=0, concat_axis=0, tiled=True)]
    ppermute x16 -> x0, waiting for transfers between devices: 15.2 us -> none  [shifted(): return lax.ppermute(shard, axis, pairs)]
  transfers between devices with their start and end apart: 24 -> 0, of which waited for: 22 -> 0; matrix products, arithmetic and copies ran while one was open for 8% -> 0% of each run, Pallas kernels for 0% -> 0%
where the time goes in v2:
time: 229 us; the launch traced here: 228 us
  Pallas kernels  210 us (92%)
  local copies, waits for them, and re-layouts  14.2 us (6%)
  matrix products  2.93 us (1%)
    pallas_call x1, Pallas kernels, mixer(): pl.pallas_call(mixer_kernel, out_shape=jax.ShapeDtypeStruct((own, model),...  115 us
    pallas_call x1, Pallas kernels, experts_of(): pl.pallas_call(expert_kernel, out_shape=jax.ShapeDtypeStruct((slots, mode...  62.7 us
    pallas_call x2, Pallas kernels, exchange(): pl.pallas_call(exchange_kernel, out_shape=jax.ShapeDtypeStruct(blocks.sha...  31.6 us
    unnamed x20, local copies, waits for them, and re-layouts  8.37 us

profile of v2, /device:TPU:1, one launch (start us, length us, event | category | flops | bytes accessed | tf_op | source)
XLA Modules:
  0.0 228.1 jit_solution(82703834497607810)
XLA Ops:
  0.0 0.8 copy.25
  0.9 0.1 fusion.1
  1.3 0.9 copy.24.sw
  2.2 0.9 copy-done.1
  3.1 0.9 copy-done.2
  4.1 0.9 copy-done.3
  5.0 0.9 copy-done.4
  6.0 0.8 copy-done.5
  6.8 0.7 copy-done.6
  7.5 0.7 copy-done.7
  8.2 0.7 copy-done.8
  8.9 115.4 %mixer.1 = bf16[8,4096]{1,0:T(8,128)(2,1)S(1)} custom-call(bf16[128,256]{1,0:T(8,128)(2,1)S(1)} %copy-done.5, bf16[256,512]{1,0:T(8,128)(2,1)S(1)} %copy-done.1, bf16[256,512]{1,0:T(8,128)(2,1)S(1)} %copy-done.2, f32[4,512]{1,0:T(4,128)S(1)} %copy-done.6, f32[1,512]{1,0:T(1,128)S(1)} %bitcast.9, bf16[512,32]{1,0:T(8,128)(2,1)S(1)} %copy.24.sw, ...), custom_call_target="tpu_custom_call" | custom-call | tf_op jit(solution)/shard_map/mixer/pallas_call | solution.py:485
  124.3 0.1 fusion.2
  124.5 0.9 fusion.6
  125.4 0.8 select_reduce_fusion.1
  126.4 1.0 convolution_convert_fusion
  127.4 0.9 reshape.55.given
  128.3 14.1 %exchange_2.1 = bf16[16,2,4096]{2,1,0:T(2,128)(2,1)} custom-call(bf16[16,2,4096]{2,1,0:T(2,128)(2,1)} %reshape.55.given), custom_call_target="tpu_custom_call" | custom-call | tf_op jit(solution)/shard_map/exchange_2/pallas_call | solution.py:751
  142.4 1.7 reshape.56.arrived
  144.1 62.7 %experts.1 = bf16[32,4096]{1,0:T(8,128)(2,1)} custom-call(bf16[32,4096]{1,0:T(8,128)(2,1)} %reshape.56.arrived, bf16[448,4096]{1,0:T(8,128)(2,1)} %bitcast.11, bf16[448,4096]{1,0:T(8,128)(2,1)} %bitcast.12, bf16[448,4096]{1,0:T(8,128)(2,1)} %bitcast.13), custom_call_target="tpu_custom_call" | custom-call | tf_op jit(solution)/shard_map/experts/pallas_call | solution.py:694
  206.8 1.8 reshape.57.given
  208.7 17.5 %exchange_3.1 = bf16[16,2,4096]{2,1,0:T(2,128)(2,1)} custom-call(bf16[16,2,4096]{2,1,0:T(2,128)(2,1)} %reshape.57.given), custom_call_target="tpu_custom_call" | custom-call | tf_op jit(solution)/shard_map/exchange_3/pallas_call | solution.py:751
  226.2 1.0 reshape.58
  227.3 0.9 fusion
  (21 shorter events, 0.5 us)
Async XLA Ops:
  0.0 124.5 %copy-start = (bf16[4096,16]{0,1:T(8,128)(2,1)S(1)}, bf16[4096,16]{0,1:T(8,128)(2,1)}, u32[]{:S(2)}) copy-start(bf16[4096,16]{0,1:T(8,128)(2,1)} %param.25) | copy-start | bytes 393220
  2.2 1.0 copy-start.1
  3.1 0.9 copy-start.2
  4.1 0.9 copy-start.3
  5.0 0.9 copy-start.4
  6.0 0.8 copy-start.5
  6.8 0.7 copy-start.6
  7.5 0.7 copy-start.7
  8.2 0.7 copy-start.8

commit v3 on v2

v3 whole, which is shorter than its diff:
```python
import functools

import jax
import jax.numpy as jnp
from jax import lax
from jax.experimental import pallas as pl
from jax.experimental.pallas import tpu as pltpu
from jax.sharding import PartitionSpec as P

STATE = 16
CONV = 4
TOP = 2
CAP = 2
SIDE = 4
PLANE = SIDE * SIDE
DEPTH = 8
EXPS = 2 * DEPTH
CHUNK = 8

precise = lax.Precision.HIGHEST
f32 = jnp.float32
bf16 = jnp.bfloat16
MESH = pl.DeviceIdType.MESH


def remote(src, dst, send_sem, recv_sem, device):
    return pltpu.make_async_remote_copy(
        src_ref=src,
        dst_ref=dst,
        send_sem=send_sem,
        recv_sem=recv_sem,
        device_id=device,
        device_id_type=MESH,
    )


def greeting(*groups):
    barrier = pltpu.get_barrier_semaphore()
    for count, device_of in groups:

        @pl.loop(1, count)
        def _(d):
            pl.semaphore_signal(barrier, inc=1, device_id=device_of(d), device_id_type=MESH)

    return lambda: pl.semaphore_wait(barrier, sum(count - 1 for count, _ in groups))


class PlaneView:
    def __init__(self, x_first):
        c, self.e = lax.axis_index("ctx"), lax.axis_index("exp")
        y, x = c // SIDE, lax.rem(c, SIDE)
        self.x_first = x_first
        self.f, self.s = (x, y) if x_first else (y, x)

    def at(self, df, ds):
        f, s = lax.rem(self.f + df + SIDE, SIDE), lax.rem(self.s + ds + SIDE, SIDE)
        return s * SIDE + f if self.x_first else f * SIDE + s


class PlaneGather:
    ORDER = (0, -1, 1, 2)

    def __init__(self, part, x_first, send, recv):
        self.view, self.part, self.send, self.recv = PlaneView(x_first), part, send, recv

    def copy(self, k, slot, which, target):
        block = self.part(slot, which)
        return remote(block, block, self.send.at[k], self.recv.at[k], (target, self.view.e))

    def sent(self, k):
        at = self.view.at
        if k < 4:
            slot, which = ((0, None), (0, None), (-1, 0), (1, 1))[k]
            return self.copy(k, at(slot, 0), which, at(1 if k % 2 == 0 else -1, 0))
        df, kind = self.ORDER[(k - 4) // 4], (k - 4) % 4
        slot, which = ((0, None), (0, None), (-1, 0), (1, 1))[kind]
        return self.copy(k, at(df, slot), which, at(0, 1 if kind % 2 == 0 else -1))

    def arrived(self, k):
        at = self.view.at
        if k < 4:
            slot, which = ((-1, None), (1, None), (2, 0), (2, 1))[k]
            return self.copy(k, at(slot, 0), which, at(0, 0))
        df, kind = self.ORDER[(k - 4) // 4], (k - 4) % 4
        slot, which = ((-1, None), (1, None), (2, 0), (2, 1))[kind]
        return self.copy(k, at(df, slot), which, at(0, 0))

    def start(self, *ks):
        for k in ks:
            self.sent(k).start()

    def await_(self, *ks):
        for k in ks:
            self.arrived(k).wait_recv()

    def finish(self, ks=range(20)):
        for k in ks:
            self.sent(k).wait_send()


def first_sends(gathers):
    for g in gathers:
        g.start(0, 1)
    for g in gathers:
        g.start(4, 5)


def first_hop(gathers):
    for g in gathers:
        g.await_(0)
        g.start(2, 8, 9)
        g.await_(1)
        g.start(3, 12, 13)


def first_axis_done(gathers):
    for g in gathers:
        g.await_(2, 3)
        g.start(16, 17)


def second_hop_of(gathers, j):
    for g in gathers:
        g.await_(4 + 4 * j)
        g.start(6 + 4 * j)
        g.await_(5 + 4 * j)
        g.start(7 + 4 * j)


def second_hop(gathers):
    for j in range(SIDE):
        second_hop_of(gathers, j)


def second_axis_done(gathers):
    for j in range(4):
        for g in gathers:
            g.await_(6 + 4 * j, 7 + 4 * j)


def rows_part(ref, begin, length):
    def part(slot, which):
        if which is None:
            return ref.at[slot, pl.ds(begin, length), :]
        return ref.at[slot, pl.ds(begin + which * (length // 2), length // 2), :]

    return part


def mixer_kernel(
    tok,
    wx,
    wz,
    cw_hbm,
    cb_hbm,
    sw_hbm,
    ss,
    sg_hbm,
    wo,
    out,
    tg,
    gw,
    go,
    cw,
    cb,
    sw,
    sg,
    steps,
    acc,
    gate,
    ext,
    tail,
    halo,
    mw,
    keep,
    cum,
    read,
    q0,
    q1,
    q2,
    q3,
    sb,
    st,
    mg,
    ml,
    part,
    pair,
    summed,
    landed,
    leave,
    fin,
    town,
    load_sem,
    x_send,
    x_recv,
    z_send,
    z_recv,
    core_send,
    core_recv,
    gw_send,
    gw_recv,
    go_send,
    go_recv,
    halo_send,
    halo_recv,
    q_send,
    q_recv,
    st_send,
    st_recv,
    mg_send,
    mg_recv,
    pair_send,
    pair_recv,
    sum_send,
    sum_recv,
    fin_send,
    fin_recv,
):
    c, e = lax.axis_index("ctx"), lax.axis_index("exp")
    y, x = c // SIDE, lax.rem(c, SIDE)
    z, core = e // 2, lax.rem(e, 2)
    partner = z * 2 + 1 - core
    rows, width = tok.shape
    lanes = wx.shape[1] // SIDE
    own_rows = out.shape[0]

    def around(value, size):
        return lax.rem(value + size, size)

    def in_row(index):
        return y * SIDE + index // 2, z * 2 + lax.rem(index, 2)

    def along_z(d):
        return c, around(z + d, DEPTH) * 2 + core

    def along_y(d):
        return around(y + d, SIDE) * SIDE + x, e

    spot = x * 2 + core
    spots = 2 * SIDE
    meet = greeting(
        (spots, lambda d: in_row(around(spot + d, spots))), (DEPTH, along_z), (SIDE, along_y)
    )

    def columns(block):
        return pl.ds(pl.multiple_of(block * lanes, lanes), lanes)

    mine = columns(x)
    loads = [
        pltpu.make_async_copy(source, place, load_sem.at[i])
        for i, (source, place) in enumerate(
            (
                (tok, tg.at[e, x]),
                (wx.at[:, mine], gw.at[c, :, pl.ds(0, lanes)]),
                (wz.at[:, mine], gw.at[c, :, pl.ds(lanes, lanes)]),
                (ss.at[:, mine], steps.at[x]),
                (cw_hbm.at[:, mine], cw),
                (cb_hbm.at[:, mine], cb),
                (sw_hbm.at[:, mine], sw),
                (sg_hbm.at[:, mine], sg),
                (wo, go.at[y]),
            )
        )
    ]
    for load in loads:
        load.start()
    meet()

    def x_copy(i, d, source, to):
        slot = y * SIDE + source
        src, dst = (
            (tok, tg.at[e, source]),
            (wx.at[:, columns(to)], gw.at[slot, :, pl.ds(0, lanes)]),
            (wz.at[:, columns(to)], gw.at[slot, :, pl.ds(lanes, lanes)]),
            (ss.at[:, columns(to)], steps.at[source]),
        )[i]
        return remote(src, dst, x_send.at[i, d], x_recv.at[i, d], (y * SIDE + to, e))

    for i in range(4):
        for d in (1, 3, 2):
            x_copy(i, d, x, around(x + d, SIDE)).start()

    def z_part(zz, s, which):
        slot = around(zz, DEPTH) * 2 + core
        if which is None:
            return tg.at[slot, s]
        return tg.at[slot, s, pl.ds(which * (rows // 2), rows // 2), :]

    def z_copy(way, hop, s, sender):
        block = sender - (hop - 1) if way == 0 else sender + (hop - 1)
        ref = z_part(block + DEPTH, s, None if hop < 4 else way)
        to = around(sender + (1 if way == 0 else -1) + DEPTH, DEPTH) * 2 + core
        return remote(ref, ref, z_send.at[way, hop - 1, s], z_recv.at[way, hop - 1, s], (c, to))

    def z_sent(way, hop, s):
        return z_copy(way, hop, s, z)

    def z_arrived(way, hop, s):
        return z_copy(way, hop, s, z - 1 if way == 0 else z + 1)

    def core_copy(zz, k):
        ref = tg.at[zz * 2 + k]
        return remote(ref, ref, core_send.at[zz], core_recv.at[zz], (c, partner))

    order = [around(x + d, SIDE) for d in PlaneGather.ORDER]
    weights = PlaneGather(
        rows_part(gw, 0, gw.shape[1]), True, gw_send, gw_recv
    )
    loads[0].wait()
    for way in range(2):
        z_sent(way, 1, x).start()
    loads[1].wait()
    loads[2].wait()
    weights.start(4, 5)
    for i, d in ((1, 1), (2, 3), (3, 2)):
        x_copy(0, d, order[i], x).wait_recv()
        for way in range(2):
            z_sent(way, 1, order[i]).start()
        x_copy(1, d, order[i], x).wait_recv()
        x_copy(2, d, order[i], x).wait_recv()
        weights.start(4 + 4 * i, 5 + 4 * i)
    core_copy(z, core).start()

    def z_hop(hop):
        for s in order:
            for way in range(2):
                z_arrived(way, hop, s).wait_recv()
                if hop < 4:
                    z_sent(way, hop + 1, s).start()
        core_copy(around(z - hop, DEPTH), core).start()
        if hop < 4:
            core_copy(around(z + hop, DEPTH), core).start()

    second_hop_of((weights,), 0)
    z_hop(1)
    second_hop_of((weights,), 1)
    second_hop_of((weights,), 2)
    z_hop(2)
    second_hop_of((weights,), 3)
    z_hop(3)
    second_axis_done((weights,))
    outs = PlaneGather(
        lambda slot, which: go.at[slot // SIDE]
        if which is None
        else go.at[slot // SIDE, pl.ds(which * (go.shape[1] // 2), go.shape[1] // 2), :],
        False,
        go_send,
        go_recv,
    )
    for load in loads[3:]:
        load.wait()
    outs.start(0, 1)
    for d in (1, 2, 3):
        x_copy(3, d, around(x - d, SIDE), x).wait_recv()
    keep[...] = jnp.exp(-jnp.concatenate([steps[s] for s in range(SIDE)], axis=1))
    z_hop(4)

    @pl.loop(0, DEPTH)
    def _(zz):
        core_copy(zz, 1 - core).wait_recv()

    acc[...] = jnp.zeros_like(acc)
    many = SIDE * rows

    @pl.loop(0, EXPS)
    def _(j):
        acc[...] += jnp.dot(tg[j].reshape(many, width), gw[j], preferred_element_type=f32)

    held = halo.shape[0]
    tail[...] = acc[pl.ds(many - held, held), pl.ds(0, lanes)].astype(bf16)

    def halo_copy():
        return remote(tail, halo, halo_send, halo_recv, along_y(1))

    @pl.when(y < SIDE - 1)
    def _():
        halo_copy().start()

    for s in range(SIDE):
        at = pl.ds(s * lanes, lanes)
        here = pl.ds(s * rows, rows)
        ext[pl.ds(held, rows), at] = acc[here, pl.ds(0, lanes)].astype(bf16).astype(f32)
        gate[:, at] = acc[here, pl.ds(lanes, lanes)].astype(bf16).astype(f32)
        if s:
            ext[pl.ds(0, held), at] = ext[pl.ds(rows, held), pl.ds((s - 1) * lanes, lanes)]

    @pl.when(y == 0)
    def _():
        halo[...] = jnp.zeros_like(halo)

    @pl.when(y > 0)
    def _():
        halo_copy().wait_recv()

    ext[pl.ds(0, held), pl.ds(0, lanes)] = halo[...].astype(f32)

    def spread(values):
        return jnp.concatenate([values] * SIDE, axis=1)

    filtered = jnp.broadcast_to(spread(cb[...]), keep.shape)
    for offset in range(CONV):
        begin = held - (CONV - 1) + offset
        tap = spread(cw[pl.ds(offset, 1), :])
        filtered = filtered + tap * ext[pl.ds(begin, rows), :]
    mixer_in = (filtered / (1.0 + jnp.exp(-filtered))).astype(bf16)
    mw[...] = mixer_in.astype(f32)

    for s in range(SIDE):
        both = lax.dot_general(
            sw[...],
            mixer_in[:, s * lanes : (s + 1) * lanes],
            (((1,), (1,)), ((), ())),
            preferred_element_type=f32,
        )
        q0[2 * s] = both[:STATE]
        q0[2 * s + 1] = both[STATE:]

    def to_sum(d, source, there):
        return remote(
            q0.at[there], q1.at[source], q_send.at[0, d], q_recv.at[0, d], in_row(there)
        )

    def z_sum(d, source):
        return remote(q2.at[source], q2.at[source], q_send.at[1, d], q_recv.at[1, d], along_z(d))

    def to_share(d, source, there):
        return remote(
            q3.at[source], q3.at[source], q_send.at[2, d], q_recv.at[2, d], in_row(there)
        )

    @pl.loop(1, spots)
    def _(d):
        to_sum(d, spot, around(spot + d, spots)).start()

    q1[spot] = q0[spot]
    outs.await_(0)
    outs.start(2)
    outs.await_(1)
    outs.start(3)

    picked = lax.broadcasted_iota(jnp.int32, (own_rows, rows), 1) == (
        lax.broadcasted_iota(jnp.int32, (own_rows, rows), 0) + e * own_rows
    )
    picker = picked.astype(f32).astype(bf16)

    @pl.loop(0, EXPS)
    def _(j):
        town[j] = jnp.dot(picker, tg[j, x], preferred_element_type=f32)

    @pl.loop(1, spots)
    def _(d):
        to_sum(d, around(spot - d, spots), spot).wait_recv()

    total = q1[0]
    for j in range(1, spots):
        total = total + q1[j]
    q2[z] = total

    @pl.loop(1, DEPTH)
    def _(d):
        z_sum(d, z).start()

    @pl.loop(1, DEPTH)
    def _(d):
        z_sum(d, around(z - d, DEPTH)).wait_recv()

    total = q2[0]
    for j in range(1, DEPTH):
        total = total + q2[j]
    q3[spot] = total

    @pl.loop(1, spots)
    def _(d):
        to_share(d, spot, around(spot + d, spots)).start()

    @pl.loop(1, spots)
    def _(d):
        to_share(d, around(spot - d, spots), spot).wait_recv()

    chunks = rows // CHUNK
    for k in range(2):
        for s in range(SIDE):
            vectors = q3[2 * s + k]
            for j in range(chunks):
                sb[j, pl.ds(k * STATE, STATE), pl.ds(s * CHUNK, CHUNK)] = vectors[
                    :, j * CHUNK : (j + 1) * CHUNK
                ]

    def advance(j, carry):
        state, decay = carry
        vectors = sb[j]
        first = pl.multiple_of(j * CHUNK, CHUNK)
        keeps, inputs = keep[pl.ds(first, CHUNK), :], mw[pl.ds(first, CHUNK), :]

        def vector(begin, i):
            picks = [
                jnp.broadcast_to(
                    vectors[begin : begin + STATE, s * CHUNK + i : s * CHUNK + i + 1],
                    (STATE, lanes),
                )
                for s in range(SIDE)
            ]
            return jnp.concatenate(picks, axis=1)

        for i in range(CHUNK):
            kept = keeps[i : i + 1, :]
            state = kept * state + inputs[i : i + 1, :] * vector(0, i)
            decay = decay * kept
            read[pl.ds(first + i, 1), :] = jnp.sum(
                vector(STATE, i) * state, axis=0, keepdims=True
            )
            cum[pl.ds(first + i, 1), :] = decay
        return state, decay

    wide = SIDE * lanes
    state, decay = lax.fori_loop(
        0, chunks, advance, (jnp.zeros((STATE, wide), f32), jnp.ones((1, wide), f32))
    )

    ends = [state[:, s * lanes : (s + 1) * lanes] for s in range(SIDE)]
    keeps = [decay[:, s * lanes : (s + 1) * lanes] for s in range(SIDE)]
    row_end, row_keep = ends[0], keeps[0]
    for s in range(1, SIDE):
        row_end, row_keep = keeps[s] * row_end + ends[s], keeps[s] * row_keep
    st[y, pl.ds(0, STATE), :] = row_end
    st[y, pl.ds(STATE, 8), :] = jnp.broadcast_to(row_keep, (8, lanes))

    def st_copy(d, slot):
        return remote(st.at[slot], st.at[slot], st_send.at[d], st_recv.at[d], along_y(d))

    @pl.loop(1, SIDE - y)
    def _(d):
        st_copy(d, y).start()

    gated = gate[...] / (1.0 + jnp.exp(-gate[...]))
    inside = read[...] + spread(sg[...]) * mw[...]

    def enter(source, entering):
        st_copy(y - source, source).wait_recv()
        return st[source, pl.ds(STATE, 1), :] * entering + st[source, pl.ds(0, STATE), :]

    entering = lax.fori_loop(0, y, enter, jnp.zeros((STATE, lanes), f32))
    carried = []
    for s in range(SIDE):
        carried.append(
            lax.dot_general(
                q3[2 * s + 1],
                entering,
                (((0,), (0,)), ((), ())),
                preferred_element_type=f32,
                precision=precise,
            )
        )
        entering = keeps[s] * entering + ends[s]
    mixed = (inside + cum[...] * jnp.concatenate(carried, axis=1)) * gated
    for s in range(SIDE):
        mg[x, s] = mixed[:, s * lanes : (s + 1) * lanes].astype(bf16)

    def mg_part(slot, which):
        at = lax.rem(slot, SIDE)
        return mg.at[at] if which is None else mg.at[at, pl.ds(which * 2, 2)]

    channels = PlaneGather(mg_part, True, mg_send, mg_recv)
    channels.start(0, 1)
    outs.await_(2, 3)
    channels.await_(0)
    channels.start(2)
    channels.await_(1)
    channels.start(3)
    channels.await_(2, 3)
    for s in range(SIDE):
        ml[:, pl.ds(s * lanes, lanes)] = mg[s].reshape(many, lanes)

    block_columns = go.shape[2]

    @pl.loop(0, SIDE)
    def _(j):
        block = jnp.dot(ml[...], go[j], preferred_element_type=f32)
        at = pl.ds(pl.multiple_of(j * block_columns, block_columns), block_columns)
        for i in range(EXPS):
            for s in range(SIDE):
                begin = s * rows + i * own_rows
                part[i % 2, i // 2, s, :, at] = block[begin : begin + own_rows].astype(bf16)

    pair_copy = remote(part.at[1 - core], pair, pair_send, pair_recv, (c, partner))
    pair_copy.start()
    pair_copy.wait_recv()

    def sum_copy(d, there, source):
        return remote(
            summed.at[there], landed.at[source], sum_send.at[d], sum_recv.at[d], along_z(d)
        )

    @pl.loop(1, DEPTH)
    def _(d):
        there = around(z + d, DEPTH)
        summed[there] = (part[core, there].astype(f32) + pair[there].astype(f32)).astype(bf16)
        sum_copy(d, there, z).start()

    def collect(d, total):
        source = around(z - d, DEPTH)
        sum_copy(d, z, source).wait_recv()
        return total + landed[source].astype(f32)

    total = lax.fori_loop(
        1, DEPTH, collect, part[core, z].astype(f32) + pair[z].astype(f32)
    )
    leave[...] = total.astype(bf16)

    def fin_copy(d, there, source):
        return remote(
            leave.at[there], fin.at[source], fin_send.at[d], fin_recv.at[d], (y * SIDE + there, e)
        )

    for d in (1, 3, 2):
        fin_copy(d, around(x + d, SIDE), x).start()
    fin[x] = leave[x]
    for d in (1, 3, 2):
        fin_copy(d, x, around(x - d, SIDE)).wait_recv()
    for i in range(SIDE):
        for s in range(SIDE):
            block = i * SIDE + s
            term = fin[s, :, pl.ds(i * block_columns, block_columns)].astype(f32)
            out[:, pl.ds(block * width, width)] = (town[block] + term).astype(bf16)

    for d in (1, 2, 3):
        for i in range(4):
            x_copy(i, d, x, around(x + d, SIDE)).wait_send()
        fin_copy(d, around(x + d, SIDE), x).wait_send()
    for s in order:
        for way in range(2):
            for hop in range(1, 5):
                z_sent(way, hop, s).wait_send()
    weights.finish(range(4, 20))
    outs.finish(range(4))
    channels.finish(range(4))

    @pl.loop(0, DEPTH)
    def _(zz):
        core_copy(zz, core).wait_send()

    @pl.when(y < SIDE - 1)
    def _():
        halo_copy().wait_send()

    @pl.loop(1, spots)
    def _(d):
        to_sum(d, spot, around(spot + d, spots)).wait_send()
        z_sum(d, z).wait_send()
        to_share(d, spot, around(spot + d, spots)).wait_send()
        sum_copy(d, around(z + d, DEPTH), z).wait_send()

    @pl.loop(1, SIDE - y)
    def _(d):
        st_copy(d, y).wait_send()

    pair_copy.wait_send()


def mixer(tokens, wx, wz, cw, cb, sw, ss, sg, wo):
    rows, width = tokens.shape
    depth, inner = wx.shape
    lanes = inner // SIDE
    model = width * EXPS
    own = rows // EXPS
    dma = pltpu.SemaphoreType.DMA
    vmem = pltpu.VMEM
    wide = vmem((rows, inner), f32)
    spread = (DEPTH, SIDE, own, model // SIDE)
    vectors = vmem((2 * SIDE, STATE, rows), f32)
    return pl.pallas_call(
        mixer_kernel,
        out_shape=jax.ShapeDtypeStruct((own, model), bf16),
        in_specs=[pl.BlockSpec(memory_space=pltpu.HBM)] * 9,
        out_specs=pl.BlockSpec(memory_space=pltpu.VMEM),
        scratch_shapes=[
            vmem((EXPS, SIDE, rows, width), bf16),
            vmem((PLANE, depth, 2 * lanes), bf16),
            vmem((SIDE, *wo.shape), bf16),
            vmem((CONV, lanes), f32),
            vmem((1, lanes), f32),
            vmem((2 * STATE, lanes), bf16),
            vmem((1, lanes), f32),
            vmem((SIDE, rows, lanes), f32),
            vmem((SIDE * rows, 2 * lanes), f32),
            wide,
            vmem((rows + 16, inner), f32),
            vmem((16, lanes), bf16),
            vmem((16, lanes), bf16),
            wide,
            wide,
            wide,
            wide,
            vectors,
            vectors,
            vmem((DEPTH, STATE, rows), f32),
            vectors,
            vmem((rows // CHUNK, 2 * STATE, 128), f32),
            vmem((SIDE, STATE + 8, lanes), f32),
            vmem((SIDE, SIDE, rows, lanes), bf16),
            vmem((SIDE * rows, inner), bf16),
            vmem((2, *spread), bf16),
            vmem(spread, bf16),
            vmem(spread, bf16),
            vmem(spread, bf16),
            vmem(spread[1:], bf16),
            vmem(spread[1:], bf16),
            vmem((EXPS, own, width), f32),
            dma((9,)),
            dma((4, SIDE)),
            dma((4, SIDE)),
            dma((2, 4, SIDE)),
            dma((2, 4, SIDE)),
            dma((DEPTH,)),
            dma((DEPTH,)),
            dma((20,)),
            dma((20,)),
            dma((4,)),
            dma((4,)),
            dma,
            dma,
            dma((3, DEPTH)),
            dma((3, DEPTH)),
            dma((SIDE,)),
            dma((SIDE,)),
            dma((4,)),
            dma((4,)),
            dma,
            dma,
            dma((DEPTH,)),
            dma((DEPTH,)),
            dma((SIDE,)),
            dma((SIDE,)),
        ],
        compiler_params=pltpu.CompilerParams(
            collective_id=0, has_side_effects=True, vmem_limit_bytes=62 << 20
        ),
        name="mixer",
    )(tokens, wx, wz, cw, cb.reshape(1, -1), sw.T, ss, sg.reshape(1, -1), wo)


class PlaneReduce:
    ORDER = (2, -1, 1, 0)

    def __init__(self, part, late, x_first, send, recv):
        self.view, self.part, self.late = PlaneView(x_first), part, late
        self.send, self.recv = send, recv

    def place(self, k, step):
        if k < 16:
            return self.view.at(self.ORDER[k // 4], step)
        return self.view.at(step, 0)

    def copy(self, k):
        kind = k % 4
        step, which, to = ((2, 0, 1), (2, 1, -1), (1, None, 1), (-1, None, -1))[kind]
        target = self.view.at(0, to) if k < 16 else self.view.at(to, 0)
        return remote(
            self.part(self.place(k, step), which),
            self.late(k, which),
            self.send.at[k],
            self.recv.at[k],
            (target, self.view.e),
        )

    def add(self, k, step, which):
        self.copy(k).wait_recv()
        mine = self.part(self.place(k, step), which)
        mine[...] = (mine[...].astype(f32) + self.late(k, which)[...].astype(f32)).astype(bf16)

    def far(self, j):
        self.copy(4 * j).start()
        self.copy(4 * j + 1).start()

    def near(self, j):
        self.add(4 * j, 1, 0)
        self.copy(4 * j + 2).start()
        self.add(4 * j + 1, -1, 1)
        self.copy(4 * j + 3).start()

    def close(self, j):
        self.add(4 * j + 2, 0, None)
        self.add(4 * j + 3, 0, None)

    def finish(self):
        for k in range(20):
            self.copy(k).wait_send()


def chunk_part(ref, row, rows, column, columns):
    def part(slot, which):
        if which is None:
            return ref.at[slot, pl.ds(row, rows), pl.ds(column, columns)]
        half = columns // 2
        return ref.at[slot, pl.ds(row, rows), pl.ds(column + which * half, half)]

    return part


def expert_kernel(
    normed,
    selector,
    combine,
    residual,
    wg_hbm,
    wu_hbm,
    wd_hbm,
    out,
    wg,
    wu,
    wd,
    give,
    take,
    back,
    ret,
    packed,
    rows_in,
    acc_g,
    acc_u,
    sums,
    late,
    load_sem,
    out_send,
    out_recv,
    back_send,
    back_recv,
    ag_send,
    ag_recv,
    rs_send,
    rs_recv,
):
    c, e = lax.axis_index("ctx"), lax.axis_index("exp")
    loads = [
        pltpu.make_async_copy(src, dst, load_sem.at[i])
        for i, (src, dst) in enumerate(((wg_hbm, wg), (wu_hbm, wu), (wd_hbm, wd)))
    ]
    for load in loads:
        load.start()
    meet = greeting(
        (PLANE, lambda d: (lax.rem(c + d, PLANE), e)), (EXPS, lambda d: (c, lax.rem(e + d, EXPS)))
    )
    slots, model = packed.shape
    units = wg.shape[0]
    turned = (((1,), (1,)), ((), ()))

    packed[...] = jnp.dot(selector[...], normed[...], preferred_element_type=f32)
    for j in range(EXPS):
        give[j] = packed[pl.ds(j * CAP, CAP), :].astype(bf16)
    take[e] = give[e]
    meet()

    def out_copy(there, source):
        return remote(
            give.at[there], take.at[source], out_send.at[there], out_recv.at[source], (c, there)
        )

    @pl.loop(1, EXPS)
    def _(d):
        out_copy(lax.rem(e + d, EXPS), e).start()

    half_rows, half_model = slots // 2, model // 2
    gathers, reduces = [], []
    for i in range(2):
        row = i * half_rows
        gathers.append(
            [
                PlaneGather(
                    chunk_part(rows_in, row, half_rows, h * half_model, half_model),
                    h == 0,
                    ag_send.at[i, h],
                    ag_recv.at[i, h],
                )
                for h in range(2)
            ]
        )

        def landing(i, h):
            def at(k, which):
                if which is None:
                    return late.at[i, h, k]
                return late.at[i, h, k, :, pl.ds(which * (half_model // 2), half_model // 2)]

            return at

        reduces.append(
            [
                PlaneReduce(
                    chunk_part(sums, row, half_rows, h * half_model, half_model),
                    landing(i, h),
                    h == 0,
                    rs_send.at[i, h],
                    rs_recv.at[i, h],
                )
                for h in range(2)
            ]
        )

    def collect(i):
        first = i * (EXPS // 2)

        @pl.loop(first, first + EXPS // 2)
        def _(j):
            @pl.when(j != e)
            def _():
                out_copy(e, j).wait_recv()

        for j in range(first, first + EXPS // 2):
            packed[pl.ds(j * CAP, CAP), :] = take[j].astype(f32)
        at = pl.ds(i * half_rows, half_rows)
        rows_in[c, at, :] = packed[at, :].astype(bf16)

    step = 512
    many = PLANE * half_rows

    def gate_up(i, begin, end):
        @pl.loop(begin, end)
        def _(k):
            at = pl.ds(pl.multiple_of(k * step, step), step)
            block = rows_in[:, pl.ds(i * half_rows, half_rows), at].reshape(many, step)
            acc_g[i] += lax.dot_general(block, wg[:, at], turned, preferred_element_type=f32)
            acc_u[i] += lax.dot_general(block, wu[:, at], turned, preferred_element_type=f32)

    def hidden_of(i):
        gate = acc_g[i]
        return ((gate / (1.0 + jnp.exp(-gate))) * acc_u[i]).astype(bf16)

    def down(i, hidden, begin, end):
        @pl.loop(begin, end)
        def _(k):
            at = pl.ds(pl.multiple_of(k * step, step), step)
            block = jnp.dot(hidden, wd[:, at], preferred_element_type=f32)
            sums[:, pl.ds(i * half_rows, half_rows), at] = block.astype(bf16).reshape(
                PLANE, half_rows, step
            )

    def give_back(i):
        for r in reduces[i]:
            r.close(4)
        packed[pl.ds(i * half_rows, half_rows), :] = sums[
            c, pl.ds(i * half_rows, half_rows), :
        ].astype(f32)
        first = i * (EXPS // 2)
        for j in range(first, first + EXPS // 2):
            back[j] = packed[pl.ds(j * CAP, CAP), :].astype(bf16)

        @pl.loop(first, first + EXPS // 2)
        def _(j):
            @pl.when(j != e)
            def _():
                back_copy(j, e).start()

            @pl.when(j == e)
            def _():
                ret[e] = back[e]

    def back_copy(there, source):
        return remote(
            back.at[there], ret.at[source], back_send.at[there], back_recv.at[source], (c, there)
        )

    first, second = gathers
    collect(0)
    first_sends(first)
    collect(1)
    first_sends(second)
    acc_g[...] = jnp.zeros_like(acc_g)
    acc_u[...] = jnp.zeros_like(acc_u)
    first_hop(first)
    first_hop(second)
    first_axis_done(first)
    first_axis_done(second)
    second_hop(first)
    second_axis_done(first)
    for load in loads:
        load.wait()
    steps = model // step
    for j in range(SIDE):
        gate_up(0, j * (steps // SIDE), (j + 1) * (steps // SIDE))
        second_hop_of(second, j)
    hidden = hidden_of(0)
    down(0, hidden, 0, steps)
    for j in range(SIDE):
        for r in reduces[0]:
            r.far(j)
    second_axis_done(second)
    for j in range(SIDE):
        gate_up(1, j * (steps // SIDE), (j + 1) * (steps // SIDE))
        for r in reduces[0]:
            r.near(j)
    hidden = hidden_of(1)
    down(1, hidden, 0, steps)
    for j in range(SIDE):
        for r in reduces[1]:
            r.far(j)
    for j in range(SIDE):
        for r in reduces[0]:
            r.close(j)
            if j == 0:
                r.far(4)
    for j in range(SIDE):
        for r in reduces[1]:
            r.near(j)
    for r in reduces[0]:
        r.near(4)
    for j in range(SIDE):
        for r in reduces[1]:
            r.close(j)
            if j == 0:
                r.far(4)
    give_back(0)
    for r in reduces[1]:
        r.near(4)
    give_back(1)

    @pl.loop(0, EXPS)
    def _(j):
        @pl.when(j != e)
        def _():
            back_copy(e, j).wait_recv()

    for j in range(EXPS):
        packed[pl.ds(j * CAP, CAP), :] = ret[j].astype(f32)
    moe = jnp.dot(combine[...], packed[...], preferred_element_type=f32, precision=precise)
    out[...] = (residual[...].astype(f32) + moe).astype(bf16)

    for pair in gathers:
        for g in pair:
            g.finish()
    for pair in reduces:
        for r in pair:
            r.finish()

    @pl.loop(1, EXPS)
    def _(d):
        there = lax.rem(e + d, EXPS)
        out_copy(there, e).wait_send()
        back_copy(there, e).wait_send()


def experts_of(normed, selector, combine, residual, wg, wu, wd):
    own, model = normed.shape
    slots = selector.shape[0]
    units = wg.shape[0]
    dma = pltpu.SemaphoreType.DMA
    vmem = pl.BlockSpec(memory_space=pltpu.VMEM)
    anywhere = pl.BlockSpec(memory_space=pltpu.HBM)
    pairs = pltpu.VMEM((EXPS, CAP, model), bf16)
    return pl.pallas_call(
        expert_kernel,
        out_shape=jax.ShapeDtypeStruct((own, model), bf16),
        in_specs=[vmem] * 4 + [anywhere] * 3,
        out_specs=vmem,
        scratch_shapes=[
            pltpu.VMEM((units, model), bf16),
            pltpu.VMEM((units, model), bf16),
            pltpu.VMEM((units, model), bf16),
            pairs,
            pairs,
            pairs,
            pairs,
            pltpu.VMEM((slots, model), f32),
            pltpu.VMEM((PLANE, slots, model), bf16),
            pltpu.VMEM((2, PLANE * slots // 2, units), f32),
            pltpu.VMEM((2, PLANE * slots // 2, units), f32),
            pltpu.VMEM((PLANE, slots, model), bf16),
            pltpu.VMEM((2, 2, 20, slots // 2, model // 2), bf16),
            dma((3,)),
            dma((EXPS,)),
            dma((EXPS,)),
            dma((EXPS,)),
            dma((EXPS,)),
            dma((2, 2, 20)),
            dma((2, 2, 20)),
            dma((2, 2, 20)),
            dma((2, 2, 20)),
        ],
        compiler_params=pltpu.CompilerParams(
            collective_id=1, has_side_effects=True, vmem_limit_bytes=62 << 20
        ),
        name="experts",
    )(normed, selector, combine, residual, wg, wu, wd)


def local(
    tokens,
    input_weight,
    gate_weight,
    conv_weight,
    conv_bias,
    state_weight,
    step_size,
    skip_gain,
    output_weight,
    norm_gain,
    router_weight,
    expert_gate,
    expert_up,
    expert_down,
    expert_ids,
):
    residual = mixer(
        tokens,
        input_weight,
        gate_weight,
        conv_weight,
        conv_bias,
        state_weight,
        step_size,
        skip_gain,
        output_weight,
    )
    row_count = expert_ids.shape[0]
    stream = residual.astype(f32)
    normed = (
        stream
        * lax.rsqrt(jnp.mean(stream * stream, -1, keepdims=True) + 1e-05)
        * norm_gain[None, :]
    ).astype(bf16)
    logits = jnp.dot(normed, router_weight, preferred_element_type=f32)
    experts = router_weight.shape[1]
    expert_range = jnp.arange(experts, dtype=jnp.int32)
    chosen = expert_ids[:, :, None] == expert_range[None, None, :]
    selected_entry = jnp.sum(jnp.where(chosen, logits[:, None, :], 0.0), -1)
    shares = jax.nn.sigmoid(selected_entry - selected_entry[:, ::-1])
    flat_hits = chosen.reshape(row_count * TOP, experts).astype(f32)
    earlier_hits = jnp.dot(
        jnp.tril(jnp.ones((row_count * TOP, row_count * TOP), f32), -1),
        flat_hits,
        precision=precise,
    )
    slot_index = jnp.sum(earlier_hits * flat_hits, -1).astype(jnp.int32)
    target = expert_ids.reshape(-1) * CAP + slot_index
    placed = target[:, None] == jnp.arange(experts * CAP, dtype=jnp.int32)[None, :]
    placed = placed.reshape(row_count, TOP, experts * CAP)
    selector = jnp.any(placed, 1).astype(bf16).T
    combine = jnp.sum(jnp.where(placed, shares[:, :, None], 0.0), 1)
    return experts_of(
        normed, selector, combine, residual, expert_gate[0], expert_up[0], expert_down[0]
    )


def solution(mesh):
    in_specs = (
        P("ctx", "exp"),
        P("ctx", "exp"),
        P("ctx", "exp"),
        P(None, "exp"),
        P("exp"),
        P("exp", None),
        P("ctx", "exp"),
        P("exp"),
        P("exp", "ctx"),
        P(),
        P(),
        P("exp", "ctx", None),
        P("exp", "ctx", None),
        P("exp", "ctx", None),
        P(("ctx", "exp"), None),
    )
    out_specs = P(("ctx", "exp"), None)
    return jax.shard_map(local, mesh=mesh, in_specs=in_specs, out_specs=out_specs, check_vma=False)
```

time: 229 us -> 179 us (0.78)
  Pallas kernels: 210 us -> 171 us
  local copies, waits for them, and re-layouts: 14.2 us -> 3.23 us
  matrix products: 2.93 us -> 0.28 us
  other arithmetic: 1.18 us -> 3.57 us
    pallas_call x1, Pallas kernels: 115 us -> 92 us  [mixer(): pl.pallas_call(mixer_kernel, out_shape=jax.ShapeDtypeStruct((own, model),...]
    pallas_call x3 -> x1, Pallas kernels: 94.3 us -> 79.1 us  [experts_of(): pl.pallas_call(expert_kernel, out_shape=jax.ShapeDtypeStruct((own, model)...]
    unnamed x20 -> x6, local copies, waits for them, and re-layouts: 8.37 us -> 2.27 us
    reshape x4 -> x0, local copies, waits for them, and re-layouts: 5.51 us -> none  [the longest x1 1.83 us: local(): returned = exchange(finished.reshape(experts, CAP, -1), 3)]
where the time goes in v3:
time: 179 us; the launch traced here: 178 us
  Pallas kernels  171 us (96%)
  other arithmetic  3.57 us (2%)
  local copies, waits for them, and re-layouts  3.23 us (2%)
    pallas_call x1, Pallas kernels, mixer(): pl.pallas_call(mixer_kernel, out_shape=jax.ShapeDtypeStruct((own, model),...  92 us
    pallas_call x1, Pallas kernels, experts_of(): pl.pallas_call(expert_kernel, out_shape=jax.ShapeDtypeStruct((own, model)...  79.1 us

profile of v3, /device:TPU:1, one launch (start us, length us, event | category | flops | bytes accessed | tf_op | source)
XLA Modules:
  0.0 178.3 jit_solution(2370854203560701156)
XLA Ops:
  0.0 0.0 copy-start
  0.0 0.8 copy.26
  0.8 0.1 eq.36
  0.9 0.1 fusion
  1.0 0.1 convert_element_type.27
  1.1 0.1 copy.28
  1.2 0.1 fusion.4
  1.3 0.7 copy.29
  2.0 92.0 %mixer.1.residual = bf16[8,4096]{1,0:T(8,128)(2,1)} custom-call(bf16[128,256]{1,0:T(8,128)(2,1)} %tok.1, bf16[256,512]{1,0:T(8,128)(2,1)} %wx.1, bf16[256,512]{1,0:T(8,128)(2,1)} %wz.1, f32[4,512]{1,0:T(4,128)} %cw_hbm.1, f32[1,512]{1,0:T(1,128)} %bitcast.14, bf16[32,512]{1,0:T(8,128)(2,1)} %bitcast.12, f32[128,512]{1,0:T(8,128)} %ss.1, f32[1,512]{1,0:T(1,128)} %bitcast.15, ...), custom_call_target="tpu_custom_call" | custom-call | tf_op jit(solution)/shard_map/mixer/pallas_call | solution.py:671
  94.0 1.0 fusion.1
  95.0 0.9 fusion.3.normed
  96.0 0.0 copy-done
  96.0 0.0 copy-start.1
  96.0 0.1 fusion.12
  96.1 0.9 select_reduce_fusion.1
  97.0 0.7 select_reduce_fusion.combine
  97.7 0.0 copy-done.1
  97.7 79.1 %experts.1 = bf16[8,4096]{1,0:T(8,128)(2,1)} custom-call(bf16[8,4096]{1,0:T(8,128)(2,1)} %copy-done.1, bf16[32,8]{1,0:T(8,128)(2,1)} %bitcast.13, f32[8,32]{1,0:T(8,128)} %select_reduce_fusion.combine, bf16[8,4096]{1,0:T(8,128)(2,1)} %mixer.1.residual, bf16[448,4096]{1,0:T(8,128)(2,1)} %bitcast.9, bf16[448,4096]{1,0:T(8,128)(2,1)} %bitcast.10, ...), custom_call_target="tpu_custom_call" | custom-call | tf_op jit(solution)/shard_map/experts/pallas_call | solution.py:1048
  176.8 1.5 copy.31
  (7 shorter events, 0.1 us)
Async XLA Ops:
  0.0 96.0 %copy-start = (bf16[4096,16]{0,1:T(8,128)(2,1)S(1)}, bf16[4096,16]{0,1:T(8,128)(2,1)}, u32[]{:S(2)}) copy-start(bf16[4096,16]{0,1:T(8,128)(2,1)} %param.25) | copy-start | bytes 393220
  96.0 1.7 copy-start.1

commit v4 on v3

v4 whole, which is shorter than its diff:
```python
import functools

import jax
import jax.numpy as jnp
from jax import lax
from jax.experimental import pallas as pl
from jax.experimental.pallas import tpu as pltpu
from jax.sharding import PartitionSpec as P

STATE = 16
CONV = 4
TOP = 2
CAP = 2
SIDE = 4
PLANE = SIDE * SIDE
DEPTH = 8
EXPS = 2 * DEPTH
CHUNK = 8

precise = lax.Precision.HIGHEST
f32 = jnp.float32
bf16 = jnp.bfloat16
MESH = pl.DeviceIdType.MESH


def remote(src, dst, send_sem, recv_sem, device):
    return pltpu.make_async_remote_copy(
        src_ref=src,
        dst_ref=dst,
        send_sem=send_sem,
        recv_sem=recv_sem,
        device_id=device,
        device_id_type=MESH,
    )


def all_sent(ref, sem):
    pltpu.make_async_copy(ref, ref, sem).wait()


def all_landed(ref, sem):
    pltpu.make_async_copy(ref, ref, sem).wait()


def greeting(*groups):
    barrier = pltpu.get_barrier_semaphore()
    for count, device_of in groups:

        @pl.loop(1, count)
        def _(d):
            pl.semaphore_signal(barrier, inc=1, device_id=device_of(d), device_id_type=MESH)

    return lambda: pl.semaphore_wait(barrier, sum(count - 1 for count, _ in groups))


class PlaneView:
    def __init__(self, x_first):
        c, self.e = lax.axis_index("ctx"), lax.axis_index("exp")
        y, x = c // SIDE, lax.rem(c, SIDE)
        self.x_first = x_first
        self.f, self.s = (x, y) if x_first else (y, x)

    def at(self, df, ds):
        f, s = lax.rem(self.f + df + SIDE, SIDE), lax.rem(self.s + ds + SIDE, SIDE)
        return s * SIDE + f if self.x_first else f * SIDE + s


class PlaneGather:
    ORDER = (0, -1, 1, 2)

    def __init__(self, part, x_first, send, recv):
        self.view, self.part, self.send, self.recv = PlaneView(x_first), part, send, recv

    def landing(self, k):
        if k < 4:
            return self.recv.at[min(k, 2)]
        j, kind = (k - 4) // 4, (k - 4) % 4
        return self.recv.at[3 + 2 * j + kind if kind < 2 else 11]

    def start(self, *ks):
        at = self.view.at
        for k in ks:
            kind = k % 4
            slot, which = ((0, None), (0, None), (-1, 0), (1, 1))[kind]
            to = 1 if kind % 2 == 0 else -1
            if k < 4:
                block, target = self.part(at(slot, 0), which), at(to, 0)
            else:
                block, target = self.part(at(self.ORDER[(k - 4) // 4], slot), which), at(0, to)
            remote(block, block, self.send, self.landing(k), (target, self.view.e)).start()

    def await_(self, k):
        all_landed(self.part(0, None), self.landing(k))

    def await_halves(self):
        all_landed(self.part(pl.ds(0, SIDE), None), self.recv.at[11])

    def finish(self, blocks):
        all_sent(blocks, self.send)


def first_sends(gathers):
    for g in gathers:
        g.start(0, 1)
    for g in gathers:
        g.start(4, 5)


def first_hop(gathers):
    for g in gathers:
        g.await_(0)
        g.start(2, 8, 9)
        g.await_(1)
        g.start(3, 12, 13)


def first_axis_done(gathers):
    for g in gathers:
        g.await_(2)
        g.start(16, 17)


def second_hop_of(gathers, j):
    for g in gathers:
        g.await_(4 + 4 * j)
        g.start(6 + 4 * j)
        g.await_(5 + 4 * j)
        g.start(7 + 4 * j)


def second_hop(gathers):
    for j in range(SIDE):
        second_hop_of(gathers, j)


def second_axis_done(gathers):
    for g in gathers:
        g.await_halves()


def rows_part(ref, begin, length):
    def part(slot, which):
        if which is None:
            return ref.at[slot, pl.ds(begin, length), :]
        return ref.at[slot, pl.ds(begin + which * (length // 2), length // 2), :]

    return part


def mix(
    tok,
    wx,
    wz,
    cw_hbm,
    cb_hbm,
    sw_hbm,
    ss,
    sg_hbm,
    wo,
    extra_loads,
    out,
    tg,
    gw,
    go,
    cw,
    cb,
    sw,
    sg,
    steps,
    acc,
    gate,
    ext,
    tail,
    halo,
    mw,
    keep,
    cum,
    read,
    q0,
    q1,
    q2,
    q3,
    sb,
    st,
    mg,
    ml,
    part,
    pair,
    summed,
    landed,
    leave,
    fin,
    town,
    stage,
    load_sem,
    tok_send,
    tok_recv,
    w_send,
    w_recv,
    ss_send,
    ss_recv,
    z_send,
    z_recv,
    core_send,
    core_recv,
    gw_send,
    gw_recv,
    go_send,
    go_recv,
    halo_send,
    halo_recv,
    q_send,
    q_recv,
    st_send,
    st_recv,
    mg_send,
    mg_recv,
    pair_send,
    pair_recv,
    sum_send,
    sum_recv,
    fin_send,
    fin_recv,
):
    c, e = lax.axis_index("ctx"), lax.axis_index("exp")
    y, x = c // SIDE, lax.rem(c, SIDE)
    z, core = e // 2, lax.rem(e, 2)
    partner = z * 2 + 1 - core
    rows, width = tok.shape
    lanes = wx.shape[1] // SIDE
    own_rows = out.shape[0]

    def around(value, size):
        return lax.rem(value + size, size)

    def first(ref, count):
        return ref.at[pl.ds(0, count)]

    def in_row(index):
        return y * SIDE + index // 2, z * 2 + lax.rem(index, 2)

    def along_z(d):
        return c, around(z + d, DEPTH) * 2 + core

    def along_y(d):
        return around(y + d, SIDE) * SIDE + x, e

    def along_x(d):
        return y * SIDE + around(x + d, SIDE), e

    spot = x * 2 + core
    spots = 2 * SIDE
    meet = greeting(
        (SIDE, along_x),
        (SIDE, along_y),
        (2, lambda d: along_z(d)),
        (2, lambda d: along_z(-d)),
        (2, lambda d: (c, partner)),
    )

    def columns(block):
        return pl.ds(pl.multiple_of(block * lanes, lanes), lanes)

    mine = columns(x)
    loads = [
        pltpu.make_async_copy(source, place, load_sem.at[i])
        for i, (source, place) in enumerate(
            (
                (tok, tg.at[e, x]),
                (wx.at[:, mine], gw.at[c, :, pl.ds(0, lanes)]),
                (wz.at[:, mine], gw.at[c, :, pl.ds(lanes, lanes)]),
                (ss.at[:, mine], steps.at[x]),
                (cw_hbm.at[:, mine], cw),
                (cb_hbm.at[:, mine], cb),
                (sw_hbm.at[:, mine], sw),
                (sg_hbm.at[:, mine], sg),
                (wo, go.at[y]),
            )
        )
    ]
    for load in loads:
        load.start()
    for load in extra_loads:
        load.start()
    meet()

    def tok_part(slot, which):
        s = slot if isinstance(slot, int) else lax.rem(slot, SIDE)
        return tg.at[e, s] if which is None else tg.at[e, s, pl.ds(which * (rows // 2), rows // 2), :]

    row_tokens = PlaneGather(tok_part, True, tok_send, tok_recv)
    deep = gw.shape[1] // 2
    sides = (pl.ds(0, lanes), pl.ds(lanes, lanes))

    def own_channels(d, part_of, place, k):
        to = columns(around(x + d, SIDE))
        hop = d if part_of is None else (1, -1)[part_of]
        at = pl.ds(0, 2 * deep) if part_of is None else pl.ds(part_of * deep, deep)
        for weight, side in zip((wx, wz), sides, strict=True):
            remote(weight.at[at, to], place.at[:, side], w_send, w_recv.at[k], along_x(hop)).start()

    for load in loads[:3]:
        load.wait()
    row_tokens.start(0, 1)

    def z_part(zz, s, which):
        slot = around(zz, DEPTH) * 2 + core
        if which is None:
            return tg.at[slot, s]
        return tg.at[slot, s, pl.ds(which * (rows // 2), rows // 2), :]

    def z_copy(way, hop, s):
        block = z - (hop - 1) if way == 0 else z + (hop - 1)
        ref = z_part(block, s, None if hop < 4 else way)
        to = around(z + (1 if way == 0 else -1), DEPTH) * 2 + core
        return remote(ref, ref, z_send, z_recv.at[hop - 1, s], (c, to))

    def z_start(hop, s):
        for way in range(2):
            z_copy(way, hop, s).start()

    def core_copy(zz):
        ref = tg.at[zz * 2 + core]
        return remote(ref, ref, core_send, core_recv, (c, partner))

    order = [around(x + d, SIDE) for d in PlaneGather.ORDER]
    weights = PlaneGather(
        rows_part(gw, 0, gw.shape[1]), True, gw_send, gw_recv
    )
    own_channels(1, None, gw.at[c], 0)
    own_channels(-1, None, gw.at[c], 1)
    own_channels(2, 0, stage.at[0], 3)
    own_channels(2, 1, stage.at[1], 4)
    z_start(1, order[0])
    weights.start(4, 5)
    row_tokens.await_(0)
    row_tokens.start(2)
    z_start(1, order[1])
    row_tokens.await_(1)
    row_tokens.start(3)
    z_start(1, order[2])
    for way in range(2):
        all_landed(stage.at[way], w_recv.at[3 + way])
        place = gw.at[y * SIDE + order[1 + way], pl.ds(way * deep, deep), :]
        remote(stage.at[way], place, w_send, w_recv.at[2], along_x((1, -1)[way])).start()
    for i in range(2):
        all_landed(gw.at[0], w_recv.at[i])
        weights.start(8 + 4 * i, 9 + 4 * i)
    row_tokens.await_(2)
    z_start(1, order[3])
    core_copy(z).start()
    all_landed(gw.at[0], w_recv.at[2])
    weights.start(16, 17)
    for d in (1, 3, 2):
        theirs = columns(around(x + d, SIDE))
        remote(ss.at[:, theirs], steps.at[x], ss_send, ss_recv, along_x(d)).start()

    def z_hop(hop):
        for s in order:
            if hop < 4:
                all_landed(tg.at[0, pl.ds(0, 2)], z_recv.at[hop - 1, s])
                z_start(hop + 1, s)
            else:
                all_landed(tg.at[0, 0], z_recv.at[hop - 1, s])
        core_copy(around(z - hop, DEPTH)).start()
        if hop < 4:
            core_copy(around(z + hop, DEPTH)).start()

    second_hop_of((weights,), 0)
    z_hop(1)
    second_hop_of((weights,), 1)
    second_hop_of((weights,), 2)
    z_hop(2)
    second_hop_of((weights,), 3)
    z_hop(3)
    second_axis_done((weights,))
    outs = PlaneGather(
        lambda slot, which: go.at[slot // SIDE]
        if which is None
        else go.at[slot // SIDE, pl.ds(which * (go.shape[1] // 2), go.shape[1] // 2), :],
        False,
        go_send,
        go_recv,
    )
    for load in loads[3:]:
        load.wait()
    outs.start(0, 1)
    all_landed(first(steps, SIDE - 1), ss_recv)
    keep[...] = jnp.exp(-jnp.concatenate([steps[s] for s in range(SIDE)], axis=1))
    z_hop(4)

    all_landed(first(tg, DEPTH), core_recv)

    acc[...] = jnp.zeros_like(acc)
    many = SIDE * rows

    @pl.loop(0, EXPS)
    def _(j):
        acc[...] += jnp.dot(tg[j].reshape(many, width), gw[j], preferred_element_type=f32)

    held = halo.shape[0]
    tail[...] = acc[pl.ds(many - held, held), pl.ds(0, lanes)].astype(bf16)

    def halo_copy():
        return remote(tail, halo, halo_send, halo_recv, along_y(1))

    @pl.when(y < SIDE - 1)
    def _():
        halo_copy().start()

    for s in range(SIDE):
        at = pl.ds(s * lanes, lanes)
        here = pl.ds(s * rows, rows)
        ext[pl.ds(held, rows), at] = acc[here, pl.ds(0, lanes)].astype(bf16).astype(f32)
        gate[:, at] = acc[here, pl.ds(lanes, lanes)].astype(bf16).astype(f32)
        if s:
            ext[pl.ds(0, held), at] = ext[pl.ds(rows, held), pl.ds((s - 1) * lanes, lanes)]

    @pl.when(y == 0)
    def _():
        halo[...] = jnp.zeros_like(halo)

    @pl.when(y > 0)
    def _():
        halo_copy().wait_recv()

    ext[pl.ds(0, held), pl.ds(0, lanes)] = halo[...].astype(f32)

    def spread(values):
        return jnp.concatenate([values] * SIDE, axis=1)

    filtered = jnp.broadcast_to(spread(cb[...]), keep.shape)
    for offset in range(CONV):
        begin = held - (CONV - 1) + offset
        tap = spread(cw[pl.ds(offset, 1), :])
        filtered = filtered + tap * ext[pl.ds(begin, rows), :]
    mixer_in = (filtered / (1.0 + jnp.exp(-filtered))).astype(bf16)
    mw[...] = mixer_in.astype(f32)

    for s in range(SIDE):
        both = lax.dot_general(
            sw[...],
            mixer_in[:, s * lanes : (s + 1) * lanes],
            (((1,), (1,)), ((), ())),
            preferred_element_type=f32,
        )
        q0[2 * s] = both[:STATE]
        q0[2 * s + 1] = both[STATE:]

    def to_sum(source, there):
        return remote(
            q0.at[there], q1.at[source], q_send.at[0], q_recv.at[0], in_row(there)
        )

    def z_sum(d, source):
        return remote(q2.at[source], q2.at[source], q_send.at[1], q_recv.at[1], along_z(d))

    def to_share(source, there):
        return remote(
            q3.at[source], q3.at[source], q_send.at[2], q_recv.at[2], in_row(there)
        )

    @pl.loop(1, spots)
    def _(d):
        to_sum(spot, around(spot + d, spots)).start()

    q1[spot] = q0[spot]
    outs.await_(0)
    outs.start(2)
    outs.await_(1)
    outs.start(3)

    picked = lax.broadcasted_iota(jnp.int32, (own_rows, rows), 1) == (
        lax.broadcasted_iota(jnp.int32, (own_rows, rows), 0) + e * own_rows
    )
    picker = picked.astype(f32).astype(bf16)

    @pl.loop(0, EXPS)
    def _(j):
        town[j] = jnp.dot(picker, tg[j, x], preferred_element_type=f32)

    all_landed(first(q1, spots - 1), q_recv.at[0])

    total = q1[0]
    for j in range(1, spots):
        total = total + q1[j]
    q2[z] = total

    @pl.loop(1, DEPTH)
    def _(d):
        z_sum(d, z).start()

    all_landed(first(q2, DEPTH - 1), q_recv.at[1])

    total = q2[0]
    for j in range(1, DEPTH):
        total = total + q2[j]
    q3[spot] = total

    @pl.loop(1, spots)
    def _(d):
        to_share(spot, around(spot + d, spots)).start()

    all_landed(first(q3, spots - 1), q_recv.at[2])

    chunks = rows // CHUNK
    for k in range(2):
        for s in range(SIDE):
            vectors = q3[2 * s + k]
            for j in range(chunks):
                sb[j, pl.ds(k * STATE, STATE), pl.ds(s * CHUNK, CHUNK)] = vectors[
                    :, j * CHUNK : (j + 1) * CHUNK
                ]

    def advance(j, carry):
        state, decay = carry
        vectors = sb[j]
        first = pl.multiple_of(j * CHUNK, CHUNK)
        keeps, inputs = keep[pl.ds(first, CHUNK), :], mw[pl.ds(first, CHUNK), :]

        def vector(begin, i):
            picks = [
                jnp.broadcast_to(
                    vectors[begin : begin + STATE, s * CHUNK + i : s * CHUNK + i + 1],
                    (STATE, lanes),
                )
                for s in range(SIDE)
            ]
            return jnp.concatenate(picks, axis=1)

        for i in range(CHUNK):
            kept = keeps[i : i + 1, :]
            state = kept * state + inputs[i : i + 1, :] * vector(0, i)
            decay = decay * kept
            read[pl.ds(first + i, 1), :] = jnp.sum(
                vector(STATE, i) * state, axis=0, keepdims=True
            )
            cum[pl.ds(first + i, 1), :] = decay
        return state, decay

    wide = SIDE * lanes
    state, decay = lax.fori_loop(
        0, chunks, advance, (jnp.zeros((STATE, wide), f32), jnp.ones((1, wide), f32))
    )

    ends = [state[:, s * lanes : (s + 1) * lanes] for s in range(SIDE)]
    keeps = [decay[:, s * lanes : (s + 1) * lanes] for s in range(SIDE)]
    row_end, row_keep = ends[0], keeps[0]
    for s in range(1, SIDE):
        row_end, row_keep = keeps[s] * row_end + ends[s], keeps[s] * row_keep
    st[y, pl.ds(0, STATE), :] = row_end
    st[y, pl.ds(STATE, 8), :] = jnp.broadcast_to(row_keep, (8, lanes))

    def st_copy(d, slot):
        return remote(st.at[slot], st.at[slot], st_send.at[d], st_recv.at[d], along_y(d))

    @pl.loop(1, SIDE - y)
    def _(d):
        st_copy(d, y).start()

    gated = gate[...] / (1.0 + jnp.exp(-gate[...]))
    inside = read[...] + spread(sg[...]) * mw[...]

    def enter(source, entering):
        st_copy(y - source, source).wait_recv()
        return st[source, pl.ds(STATE, 1), :] * entering + st[source, pl.ds(0, STATE), :]

    entering = lax.fori_loop(0, y, enter, jnp.zeros((STATE, lanes), f32))
    carried = []
    for s in range(SIDE):
        carried.append(
            lax.dot_general(
                q3[2 * s + 1],
                entering,
                (((0,), (0,)), ((), ())),
                preferred_element_type=f32,
                precision=precise,
            )
        )
        entering = keeps[s] * entering + ends[s]
    mixed = (inside + cum[...] * jnp.concatenate(carried, axis=1)) * gated
    for s in range(SIDE):
        mg[x, s] = mixed[:, s * lanes : (s + 1) * lanes].astype(bf16)

    def mg_part(slot, which):
        at = slot if isinstance(slot, int) else lax.rem(slot, SIDE)
        return mg.at[at] if which is None else mg.at[at, pl.ds(which * 2, 2)]

    channels = PlaneGather(mg_part, True, mg_send, mg_recv)
    channels.start(0, 1)
    outs.await_(2)
    channels.await_(0)
    channels.start(2)
    channels.await_(1)
    channels.start(3)
    channels.await_(2)
    for s in range(SIDE):
        ml[:, pl.ds(s * lanes, lanes)] = mg[s].reshape(many, lanes)

    block_columns = go.shape[2]
    halves = [pl.ds(h * 2 * block_columns, 2 * block_columns) for h in range(2)]

    def pair_copy(h):
        return remote(
            part.at[1 - core, :, :, :, halves[h]],
            pair.at[:, :, :, halves[h]],
            pair_send.at[h],
            pair_recv.at[h],
            (c, partner),
        )

    def sum_copy(h, d, there, source):
        return remote(
            summed.at[there, :, :, halves[h]],
            landed.at[source, :, :, halves[h]],
            sum_send.at[h],
            sum_recv.at[h],
            along_z(d),
        )

    def both_cores(h, there):
        at = halves[h]
        return part[core, there, :, :, at].astype(f32) + pair[there, :, :, at].astype(f32)

    for h in range(2):

        @pl.loop(2 * h, 2 * h + 2)
        def _(j):
            block = jnp.dot(ml[...], go[j], preferred_element_type=f32)
            at = pl.ds(pl.multiple_of(j * block_columns, block_columns), block_columns)
            for i in range(EXPS):
                for s in range(SIDE):
                    begin = s * rows + i * own_rows
                    part[i % 2, i // 2, s, :, at] = block[begin : begin + own_rows].astype(bf16)

        pair_copy(h).start()
    for h in range(2):
        pair_copy(h).wait_recv()

        @pl.loop(1, DEPTH)
        def _(d):
            there = around(z + d, DEPTH)
            summed[there, :, :, halves[h]] = both_cores(h, there).astype(bf16)
            sum_copy(h, d, there, z).start()

    for h in range(2):

        def collect(d, total):
            return total + landed[around(z - d, DEPTH), :, :, halves[h]].astype(f32)

        all_landed(landed.at[pl.ds(0, DEPTH - 1), :, :, halves[h]], sum_recv.at[h])
        total = lax.fori_loop(1, DEPTH, collect, both_cores(h, z))
        leave[:, :, halves[h]] = total.astype(bf16)

    def fin_copy(there, source):
        return remote(
            leave.at[there], fin.at[source], fin_send, fin_recv, (y * SIDE + there, e)
        )

    for d in (1, 3, 2):
        fin_copy(around(x + d, SIDE), x).start()
    fin[x] = leave[x]
    all_landed(first(fin, SIDE - 1), fin_recv)
    for i in range(SIDE):
        for s in range(SIDE):
            block = i * SIDE + s
            term = fin[s, :, pl.ds(i * block_columns, block_columns)].astype(f32)
            out[:, pl.ds(block * width, width)] = (town[block] + term).astype(bf16)

    row_tokens.finish(tg.at[e, pl.ds(0, SIDE - 1)])
    all_sent(first(gw, SIDE), w_send)
    all_sent(first(steps, SIDE - 1), ss_send)
    all_sent(first(tg, DEPTH - 1), z_send)
    all_sent(first(tg, DEPTH), core_send)
    weights.finish(first(gw, 12))
    outs.finish(first(go, SIDE - 1))
    channels.finish(first(mg, SIDE - 1))
    all_sent(first(q0, spots - 1), q_send.at[0])
    all_sent(first(q2, DEPTH - 1), q_send.at[1])
    all_sent(first(q3, spots - 1), q_send.at[2])
    for h in range(2):
        all_sent(summed.at[pl.ds(0, DEPTH - 1), :, :, halves[h]], sum_send.at[h])
        pair_copy(h).wait_send()
    all_sent(first(leave, SIDE - 1), fin_send)

    @pl.when(y < SIDE - 1)
    def _():
        halo_copy().wait_send()

    @pl.loop(1, SIDE - y)
    def _(d):
        st_copy(d, y).wait_send()


def mix_scratch(rows, width, depth, inner):
    lanes = inner // SIDE
    model = width * EXPS
    own = rows // EXPS
    dma = pltpu.SemaphoreType.DMA
    vmem = pltpu.VMEM
    wide = vmem((rows, inner), f32)
    spread = (DEPTH, SIDE, own, model // SIDE)
    vectors = vmem((2 * SIDE, STATE, rows), f32)
    return [
        vmem((EXPS, SIDE, rows, width), bf16),
        vmem((PLANE, depth, 2 * lanes), bf16),
        vmem((SIDE, inner, width), bf16),
        vmem((CONV, lanes), f32),
        vmem((1, lanes), f32),
        vmem((2 * STATE, lanes), bf16),
        vmem((1, lanes), f32),
        vmem((SIDE, rows, lanes), f32),
        vmem((SIDE * rows, 2 * lanes), f32),
        wide,
        vmem((rows + 16, inner), f32),
        vmem((16, lanes), bf16),
        vmem((16, lanes), bf16),
        wide,
        wide,
        wide,
        wide,
        vectors,
        vectors,
        vmem((DEPTH, STATE, rows), f32),
        vectors,
        vmem((rows // CHUNK, 2 * STATE, 128), f32),
        vmem((SIDE, STATE + 8, lanes), f32),
        vmem((SIDE, SIDE, rows, lanes), bf16),
        vmem((SIDE * rows, inner), bf16),
        vmem((2, *spread), bf16),
        vmem(spread, bf16),
        vmem(spread, bf16),
        vmem(spread, bf16),
        vmem(spread[1:], bf16),
        vmem(spread[1:], bf16),
        vmem((EXPS, own, width), f32),
        vmem((2, depth // 2, 2 * lanes), bf16),
        dma((9,)),
        dma,
        dma((3,)),
        dma,
        dma((5,)),
        dma,
        dma,
        dma,
        dma((4, SIDE)),
        dma,
        dma,
        dma,
        dma((12,)),
        dma,
        dma((3,)),
        dma,
        dma,
        dma((3,)),
        dma((3,)),
        dma((SIDE,)),
        dma((SIDE,)),
        dma,
        dma((3,)),
        dma((2,)),
        dma((2,)),
        dma((2,)),
        dma((2,)),
        dma,
        dma,
    ]


class PlaneReduce:
    ORDER = (2, -1, 1, 0)

    def __init__(self, part, late, x_first, send, recv):
        self.view, self.part, self.late = PlaneView(x_first), part, late
        self.send, self.recv = send, recv

    def mine(self, j, step, which):
        at = self.view.at
        return self.part(at(self.ORDER[j], step) if j < 4 else at(step, 0), which)

    def start(self, k):
        j, kind = k // 4, k % 4
        step, which, to = ((2, 0, 1), (2, 1, -1), (1, None, 1), (-1, None, -1))[kind]
        target = self.view.at(0, to) if j < 4 else self.view.at(to, 0)
        source, place = self.mine(j, step, which), self.late(k, which)
        remote(source, place, self.send, self.recv.at[k // 2], (target, self.view.e)).start()

    def far(self, j):
        self.start(4 * j)
        self.start(4 * j + 1)

    def near(self, j):
        all_landed(self.late(4 * j, None), self.recv.at[2 * j])
        for kind, step in ((0, 1), (1, -1)):
            mine, came = self.mine(j, step, kind), self.late(4 * j + kind, kind)
            mine[...] = (mine[...].astype(f32) + came[...].astype(f32)).astype(bf16)
            self.start(4 * j + 2 + kind)

    def close(self, j):
        all_landed(self.late(pl.ds(4 * j + 2, 2), None), self.recv.at[2 * j + 1])
        mine, first, second = self.mine(j, 0, None), self.late(4 * j + 2, None), self.late(4 * j + 3, None)
        total = first[...].astype(f32) + second[...].astype(f32)
        mine[...] = (mine[...].astype(f32) + total).astype(bf16)

    def finish(self):
        all_sent(self.part(pl.ds(0, 15), None), self.send)


def chunk_part(ref, row, rows, column, columns):
    def part(slot, which):
        if which is None:
            return ref.at[slot, pl.ds(row, rows), pl.ds(column, columns)]
        half = columns // 2
        return ref.at[slot, pl.ds(row, rows), pl.ds(column + which * half, half)]

    return part


def route(residual, norm_gain, router, ids):
    stream = residual[...].astype(f32)
    scale = lax.rsqrt(jnp.mean(stream * stream, axis=1, keepdims=True) + 1e-05)
    normed = (stream * scale * norm_gain[...]).astype(bf16)
    logits = lax.dot_general(
        router[...], normed, (((1,), (1,)), ((), ())), preferred_element_type=f32
    )
    experts, rows = logits.shape
    expert = lax.broadcasted_iota(jnp.int32, (experts, rows), 0)
    slot = lax.broadcasted_iota(jnp.int32, (experts * CAP, rows), 0).astype(f32)
    before = lax.broadcasted_iota(jnp.int32, (rows, rows), 0) < lax.broadcasted_iota(
        jnp.int32, (rows, rows), 1
    )
    named = [ids[pl.ds(k, 1), :] for k in range(TOP)]
    hits = [(expert == one).astype(f32) for one in named]
    earlier = jnp.dot(
        hits[0] + hits[1], before.astype(f32), preferred_element_type=f32, precision=precise
    )
    picked = [jnp.sum(hit * logits, axis=0, keepdims=True) for hit in hits]
    selector = jnp.zeros(slot.shape, f32)
    combine = jnp.zeros(slot.shape, f32)
    for k in range(TOP):
        rank = jnp.sum(hits[k] * earlier, axis=0, keepdims=True)
        placed = (slot == named[k].astype(f32) * CAP + rank).astype(f32)
        share = 1.0 / (1.0 + jnp.exp(picked[1 - k] - picked[k]))
        selector = selector + placed
        combine = combine + placed * share
    return normed, selector.astype(bf16), combine


def run_experts(
    residual,
    norm_gain,
    router,
    ids,
    loads,
    out,
    wg,
    wu,
    wd,
    give,
    take,
    back,
    ret,
    packed,
    rows_in,
    acc_g,
    acc_u,
    sums,
    late,
    out_send,
    out_recv,
    back_send,
    back_recv,
    ag_send,
    ag_recv,
    rs_send,
    rs_recv,
):
    c, e = lax.axis_index("ctx"), lax.axis_index("exp")
    slots, model = packed.shape
    turned = (((1,), (1,)), ((), ()))

    for load in loads[3:]:
        load.wait()
    normed, selector, combine = route(residual, norm_gain, router, ids)
    packed[...] = jnp.dot(selector, normed, preferred_element_type=f32)
    for j in range(EXPS):
        give[j] = packed[pl.ds(j * CAP, CAP), :].astype(bf16)
    take[e] = give[e]

    def out_copy(there, source):
        return remote(
            give.at[there], take.at[source], out_send, out_recv.at[source // (EXPS // 2)], (c, there)
        )

    @pl.loop(1, EXPS)
    def _(d):
        out_copy(lax.rem(e + d, EXPS), e).start()

    half_rows, half_model = slots // 2, model // 2
    gathers, reduces = [], []
    for i in range(2):
        row = i * half_rows
        gathers.append(
            [
                PlaneGather(
                    chunk_part(rows_in, row, half_rows, h * half_model, half_model),
                    h == 0,
                    ag_send.at[i, h],
                    ag_recv.at[i, h],
                )
                for h in range(2)
            ]
        )

        def landing(i, h):
            def at(k, which):
                if which is None:
                    return late.at[i, h, k]
                return late.at[i, h, k, :, pl.ds(which * (half_model // 2), half_model // 2)]

            return at

        reduces.append(
            [
                PlaneReduce(
                    chunk_part(sums, row, half_rows, h * half_model, half_model),
                    landing(i, h),
                    h == 0,
                    rs_send.at[i, h],
                    rs_recv.at[i, h],
                )
                for h in range(2)
            ]
        )

    def collect(i):
        first = i * (EXPS // 2)

        @pl.when(e // (EXPS // 2) == i)
        def _():
            all_landed(take.at[pl.ds(0, EXPS // 2 - 1)], out_recv.at[i])

        @pl.when(e // (EXPS // 2) != i)
        def _():
            all_landed(take.at[pl.ds(0, EXPS // 2)], out_recv.at[i])

        for j in range(first, first + EXPS // 2):
            packed[pl.ds(j * CAP, CAP), :] = take[j].astype(f32)
        at = pl.ds(i * half_rows, half_rows)
        rows_in[c, at, :] = packed[at, :].astype(bf16)

    step = 512
    many = PLANE * half_rows

    def gate_up(i, begin, end):
        @pl.loop(begin, end)
        def _(k):
            at = pl.ds(pl.multiple_of(k * step, step), step)
            block = rows_in[:, pl.ds(i * half_rows, half_rows), at].reshape(many, step)
            acc_g[i] += lax.dot_general(block, wg[:, at], turned, preferred_element_type=f32)
            acc_u[i] += lax.dot_general(block, wu[:, at], turned, preferred_element_type=f32)

    def hidden_of(i):
        gate = acc_g[i]
        return ((gate / (1.0 + jnp.exp(-gate))) * acc_u[i]).astype(bf16)

    def down(i, hidden, begin, end):
        @pl.loop(begin, end)
        def _(k):
            at = pl.ds(pl.multiple_of(k * step, step), step)
            block = jnp.dot(hidden, wd[:, at], preferred_element_type=f32)
            sums[:, pl.ds(i * half_rows, half_rows), at] = block.astype(bf16).reshape(
                PLANE, half_rows, step
            )

    def give_back(i):
        for r in reduces[i]:
            r.close(4)
        packed[pl.ds(i * half_rows, half_rows), :] = sums[
            c, pl.ds(i * half_rows, half_rows), :
        ].astype(f32)
        first = i * (EXPS // 2)
        for j in range(first, first + EXPS // 2):
            back[j] = packed[pl.ds(j * CAP, CAP), :].astype(bf16)

        @pl.loop(first, first + EXPS // 2)
        def _(j):
            @pl.when(j != e)
            def _():
                back_copy(j, e).start()

            @pl.when(j == e)
            def _():
                ret[e] = back[e]

    def back_copy(there, source):
        return remote(
            back.at[there], ret.at[source], back_send, back_recv, (c, there)
        )

    first, second = gathers
    collect(0)
    first_sends(first)
    collect(1)
    first_sends(second)
    acc_g[...] = jnp.zeros_like(acc_g)
    acc_u[...] = jnp.zeros_like(acc_u)
    first_hop(first)
    first_hop(second)
    first_axis_done(first)
    first_axis_done(second)
    second_hop(first)
    second_axis_done(first)
    for load in loads[:3]:
        load.wait()
    steps = model // step
    for j in range(SIDE):
        gate_up(0, j * (steps // SIDE), (j + 1) * (steps // SIDE))
        second_hop_of(second, j)
    hidden = hidden_of(0)
    down(0, hidden, 0, steps)
    for j in range(SIDE):
        for r in reduces[0]:
            r.far(j)
    second_axis_done(second)
    for j in range(SIDE):
        gate_up(1, j * (steps // SIDE), (j + 1) * (steps // SIDE))
        for r in reduces[0]:
            r.near(j)
    hidden = hidden_of(1)
    down(1, hidden, 0, steps)
    for j in range(SIDE):
        for r in reduces[1]:
            r.far(j)
    for j in range(SIDE):
        for r in reduces[0]:
            r.close(j)
            if j == 0:
                r.far(4)
    for j in range(SIDE):
        for r in reduces[1]:
            r.near(j)
    for r in reduces[0]:
        r.near(4)
    for j in range(SIDE):
        for r in reduces[1]:
            r.close(j)
            if j == 0:
                r.far(4)
    give_back(0)
    for r in reduces[1]:
        r.near(4)
    give_back(1)

    all_landed(ret.at[pl.ds(0, EXPS - 1)], back_recv)
    for j in range(EXPS):
        packed[pl.ds(j * CAP, CAP), :] = ret[j].astype(f32)
    moe = lax.dot_general(
        combine,
        packed[...],
        (((0,), (0,)), ((), ())),
        preferred_element_type=f32,
        precision=precise,
    )
    out[...] = (residual[...].astype(f32) + moe).astype(bf16)

    for pair in gathers:
        for g in pair:
            g.finish(g.part(pl.ds(0, 15), None))
    for pair in reduces:
        for r in pair:
            r.finish()
    all_sent(give.at[pl.ds(0, EXPS - 1)], out_send)
    all_sent(back.at[pl.ds(0, EXPS - 1)], back_send)


def expert_scratch(units, model):
    slots = EXPS * CAP
    dma = pltpu.SemaphoreType.DMA
    vmem = pltpu.VMEM
    weight = vmem((units, model), bf16)
    pairs = vmem((EXPS, CAP, model), bf16)
    return [
        weight,
        weight,
        weight,
        pairs,
        pairs,
        pairs,
        pairs,
        vmem((slots, model), f32),
        vmem((PLANE, slots, model), bf16),
        vmem((2, PLANE * slots // 2, units), f32),
        vmem((2, PLANE * slots // 2, units), f32),
        vmem((PLANE, slots, model), bf16),
        vmem((2, 2, 20, slots // 2, model // 2), bf16),
        dma,
        dma((2,)),
        dma,
        dma,
        dma((2, 2)),
        dma((2, 2, 12)),
        dma((2, 2)),
        dma((2, 2, 10)),
    ]


def layer_kernel(mix_count, *refs):
    mix_ins, (gain_hbm, router_hbm, wg_hbm, wu_hbm, wd_hbm, ids_hbm), out = refs[:9], refs[9:15], refs[15]
    residual, gain, router, ids, load_sem = refs[16:21]
    mix_refs, expert_refs = refs[21 : 21 + mix_count], refs[21 + mix_count :]
    loads = [
        pltpu.make_async_copy(source, place, load_sem.at[i])
        for i, (source, place) in enumerate(
            zip(
                (wg_hbm, wu_hbm, wd_hbm, gain_hbm, router_hbm, ids_hbm),
                (*expert_refs[:3], gain, router, ids),
                strict=True,
            )
        )
    ]
    mix(*mix_ins, loads, residual, *mix_refs)
    run_experts(residual, gain, router, ids, loads, out, *expert_refs)


def local(
    tokens,
    input_weight,
    gate_weight,
    conv_weight,
    conv_bias,
    state_weight,
    step_size,
    skip_gain,
    output_weight,
    norm_gain,
    router_weight,
    expert_gate,
    expert_up,
    expert_down,
    expert_ids,
):
    own, model = expert_ids.shape[0], norm_gain.shape[0]
    units, experts = expert_gate.shape[1], router_weight.shape[1]
    scratch = mix_scratch(*tokens.shape, *input_weight.shape)
    vmem = pltpu.VMEM
    return pl.pallas_call(
        functools.partial(layer_kernel, len(scratch)),
        out_shape=jax.ShapeDtypeStruct((own, model), bf16),
        in_specs=[pl.BlockSpec(memory_space=pltpu.HBM)] * 15,
        out_specs=pl.BlockSpec(memory_space=pltpu.VMEM),
        scratch_shapes=[
            vmem((own, model), bf16),
            vmem((1, model), f32),
            vmem((experts, model), bf16),
            vmem((TOP, own), jnp.int32),
            pltpu.SemaphoreType.DMA((6,)),
            *scratch,
            *expert_scratch(units, model),
        ],
        compiler_params=pltpu.CompilerParams(
            collective_id=0, has_side_effects=True, vmem_limit_bytes=62 << 20
        ),
        name="layer",
    )(
        tokens,
        input_weight,
        gate_weight,
        conv_weight,
        conv_bias.reshape(1, -1),
        state_weight.T,
        step_size,
        skip_gain.reshape(1, -1),
        output_weight,
        norm_gain.reshape(1, -1),
        router_weight.T,
        expert_gate[0],
        expert_up[0],
        expert_down[0],
        expert_ids.T,
    )


def solution(mesh):
    in_specs = (
        P("ctx", "exp"),
        P("ctx", "exp"),
        P("ctx", "exp"),
        P(None, "exp"),
        P("exp"),
        P("exp", None),
        P("ctx", "exp"),
        P("exp"),
        P("exp", "ctx"),
        P(),
        P(),
        P("exp", "ctx", None),
        P("exp", "ctx", None),
        P("exp", "ctx", None),
        P(("ctx", "exp"), None),
    )
    out_specs = P(("ctx", "exp"), None)
    return jax.shard_map(local, mesh=mesh, in_specs=in_specs, out_specs=out_specs, check_vma=False)
```

time: 179 us -> 161 us (0.90)
  Pallas kernels: 171 us -> 160 us
  other arithmetic: 3.57 us -> 0 us
    pallas_call x2 -> x1, Pallas kernels: 171 us -> 160 us  [local(): pl.pallas_call(functools.partial(layer_kernel, len(scratch)), out_shape=j...]
    reduce_sum x3 -> x0, other arithmetic: 2.52 us -> none  [the longest x1 0.99 us: local(): jnp.mean(stream * stream, -1, keepdims=True) + 1e-05]
where the time goes in v4:
time: 161 us
  Pallas kernels  160 us (99%)
    pallas_call x1, Pallas kernels, local(): pl.pallas_call(functools.partial(layer_kernel, len(scratch)), out_shape=j...  160 us

profile of v4, /device:TPU:1, one launch (start us, length us, event | category | flops | bytes accessed | tf_op | source)
XLA Modules:
  0.0 161.0 jit_solution(6780926849969390909)
XLA Ops:
  0.0 159.5 %layer.1 = bf16[8,4096]{1,0:T(8,128)(2,1)} custom-call(bf16[128,256]{1,0:T(8,128)(2,1)} %refs_0_.1, bf16[256,512]{1,0:T(8,128)(2,1)} %refs_1_.1, bf16[256,512]{1,0:T(8,128)(2,1)} %refs_2_.1, f32[4,512]{1,0:T(4,128)} %refs_3_.1, f32[1,512]{1,0:T(1,128)} %bitcast.15, bf16[32,512]{1,0:T(8,128)(2,1)} %bitcast.13, f32[128,512]{1,0:T(8,128)} %refs_6_.1, ...), custom_call_target="tpu_custom_call" | custom-call | tf_op jit(solution)/shard_map/layer/pallas_call | solution.py:1147
  159.5 1.5 copy.17

commit v5 on v4

--- a/solution.py
+++ b/solution.py
@@ -191,7 +191,6 @@
     leave,
     fin,
     town,
-    stage,
     load_sem,
     tok_send,
     tok_recv,
@@ -284,24 +283,15 @@
         load.start()
     meet()
 
-    def tok_part(slot, which):
-        s = slot if isinstance(slot, int) else lax.rem(slot, SIDE)
-        return tg.at[e, s] if which is None else tg.at[e, s, pl.ds(which * (rows // 2), rows // 2), :]
-
-    row_tokens = PlaneGather(tok_part, True, tok_send, tok_recv)
-    deep = gw.shape[1] // 2
-    sides = (pl.ds(0, lanes), pl.ds(lanes, lanes))
-
-    def own_channels(d, part_of, place, k):
-        to = columns(around(x + d, SIDE))
-        hop = d if part_of is None else (1, -1)[part_of]
-        at = pl.ds(0, 2 * deep) if part_of is None else pl.ds(part_of * deep, deep)
-        for weight, side in zip((wx, wz), sides, strict=True):
-            remote(weight.at[at, to], place.at[:, side], w_send, w_recv.at[k], along_x(hop)).start()
-
     for load in loads[:3]:
         load.wait()
-    row_tokens.start(0, 1)
+    for d in (2, 1, 3):
+        remote(tg.at[e, x], tg.at[e, x], tok_send, tok_recv.at[d - 1], along_x(d)).start()
+    for d in (1, 3, 2):
+        theirs = columns(around(x + d, SIDE))
+        for i, weight in enumerate((wx, wz)):
+            place = gw.at[c, :, pl.ds(i * lanes, lanes)]
+            remote(weight.at[:, theirs], place, w_send, w_recv.at[d - 1], along_x(d)).start()
 
     def z_part(zz, s, which):
         slot = around(zz, DEPTH) * 2 + core
@@ -327,30 +317,15 @@
     weights = PlaneGather(
         rows_part(gw, 0, gw.shape[1]), True, gw_send, gw_recv
     )
-    own_channels(1, None, gw.at[c], 0)
-    own_channels(-1, None, gw.at[c], 1)
-    own_channels(2, 0, stage.at[0], 3)
-    own_channels(2, 1, stage.at[1], 4)
     z_start(1, order[0])
     weights.start(4, 5)
-    row_tokens.await_(0)
-    row_tokens.start(2)
-    z_start(1, order[1])
-    row_tokens.await_(1)
-    row_tokens.start(3)
-    z_start(1, order[2])
-    for way in range(2):
-        all_landed(stage.at[way], w_recv.at[3 + way])
-        place = gw.at[y * SIDE + order[1 + way], pl.ds(way * deep, deep), :]
-        remote(stage.at[way], place, w_send, w_recv.at[2], along_x((1, -1)[way])).start()
-    for i in range(2):
-        all_landed(gw.at[0], w_recv.at[i])
-        weights.start(8 + 4 * i, 9 + 4 * i)
-    row_tokens.await_(2)
-    z_start(1, order[3])
+    for i, d in ((1, 1), (2, 3), (3, 2)):
+        all_landed(tg.at[0, 0], tok_recv.at[d - 1])
+        z_start(1, order[i])
     core_copy(z).start()
-    all_landed(gw.at[0], w_recv.at[2])
-    weights.start(16, 17)
+    for i, d in ((1, 1), (2, 3), (3, 2)):
+        all_landed(gw.at[0], w_recv.at[d - 1])
+        weights.start(4 + 4 * i, 5 + 4 * i)
     for d in (1, 3, 2):
         theirs = columns(around(x + d, SIDE))
         remote(ss.at[:, theirs], steps.at[x], ss_send, ss_recv, along_x(d)).start()
@@ -582,28 +557,20 @@
     for s in range(SIDE):
         mg[x, s] = mixed[:, s * lanes : (s + 1) * lanes].astype(bf16)
 
-    def mg_part(slot, which):
-        at = slot if isinstance(slot, int) else lax.rem(slot, SIDE)
-        return mg.at[at] if which is None else mg.at[at, pl.ds(which * 2, 2)]
-
-    channels = PlaneGather(mg_part, True, mg_send, mg_recv)
-    channels.start(0, 1)
+    for d in (2, 1, 3):
+        remote(mg.at[x], mg.at[x], mg_send, mg_recv, along_x(d)).start()
     outs.await_(2)
-    channels.await_(0)
-    channels.start(2)
-    channels.await_(1)
-    channels.start(3)
-    channels.await_(2)
+    all_landed(first(mg, SIDE - 1), mg_recv)
     for s in range(SIDE):
         ml[:, pl.ds(s * lanes, lanes)] = mg[s].reshape(many, lanes)
 
     block_columns = go.shape[2]
-    halves = [pl.ds(h * 2 * block_columns, 2 * block_columns) for h in range(2)]
+    pieces = [pl.ds(h * block_columns, block_columns) for h in range(SIDE)]
 
     def pair_copy(h):
         return remote(
-            part.at[1 - core, :, :, :, halves[h]],
-            pair.at[:, :, :, halves[h]],
+            part.at[1 - core, :, :, :, pieces[h]],
+            pair.at[:, :, :, pieces[h]],
             pair_send.at[h],
             pair_recv.at[h],
             (c, partner),
@@ -611,46 +578,41 @@
 
     def sum_copy(h, d, there, source):
         return remote(
-            summed.at[there, :, :, halves[h]],
-            landed.at[source, :, :, halves[h]],
+            summed.at[there, :, :, pieces[h]],
+            landed.at[source, :, :, pieces[h]],
             sum_send.at[h],
             sum_recv.at[h],
             along_z(d),
         )
 
     def both_cores(h, there):
-        at = halves[h]
+        at = pieces[h]
         return part[core, there, :, :, at].astype(f32) + pair[there, :, :, at].astype(f32)
 
-    for h in range(2):
-
-        @pl.loop(2 * h, 2 * h + 2)
-        def _(j):
-            block = jnp.dot(ml[...], go[j], preferred_element_type=f32)
-            at = pl.ds(pl.multiple_of(j * block_columns, block_columns), block_columns)
-            for i in range(EXPS):
-                for s in range(SIDE):
-                    begin = s * rows + i * own_rows
-                    part[i % 2, i // 2, s, :, at] = block[begin : begin + own_rows].astype(bf16)
-
+    for h in range(SIDE):
+        block = jnp.dot(ml[...], go[h], preferred_element_type=f32)
+        for i in range(EXPS):
+            for s in range(SIDE):
+                begin = s * rows + i * own_rows
+                part[i % 2, i // 2, s, :, pieces[h]] = block[begin : begin + own_rows].astype(bf16)
         pair_copy(h).start()
-    for h in range(2):
+    for h in range(SIDE):
         pair_copy(h).wait_recv()
 
         @pl.loop(1, DEPTH)
         def _(d):
             there = around(z + d, DEPTH)
-            summed[there, :, :, halves[h]] = both_cores(h, there).astype(bf16)
+            summed[there, :, :, pieces[h]] = both_cores(h, there).astype(bf16)
             sum_copy(h, d, there, z).start()
 
-    for h in range(2):
+    for h in range(SIDE):
 
         def collect(d, total):
-            return total + landed[around(z - d, DEPTH), :, :, halves[h]].astype(f32)
-
-        all_landed(landed.at[pl.ds(0, DEPTH - 1), :, :, halves[h]], sum_recv.at[h])
+            return total + landed[around(z - d, DEPTH), :, :, pieces[h]].astype(f32)
+
+        all_landed(landed.at[pl.ds(0, DEPTH - 1), :, :, pieces[h]], sum_recv.at[h])
         total = lax.fori_loop(1, DEPTH, collect, both_cores(h, z))
-        leave[:, :, halves[h]] = total.astype(bf16)
+        leave[:, :, pieces[h]] = total.astype(bf16)
 
     def fin_copy(there, source):
         return remote(
@@ -667,19 +629,19 @@
             term = fin[s, :, pl.ds(i * block_columns, block_columns)].astype(f32)
             out[:, pl.ds(block * width, width)] = (town[block] + term).astype(bf16)
 
-    row_tokens.finish(tg.at[e, pl.ds(0, SIDE - 1)])
-    all_sent(first(gw, SIDE), w_send)
+    all_sent(tg.at[0, pl.ds(0, SIDE - 1)], tok_send)
+    all_sent(first(gw, SIDE - 1), w_send)
     all_sent(first(steps, SIDE - 1), ss_send)
     all_sent(first(tg, DEPTH - 1), z_send)
     all_sent(first(tg, DEPTH), core_send)
     weights.finish(first(gw, 12))
     outs.finish(first(go, SIDE - 1))
-    channels.finish(first(mg, SIDE - 1))
+    all_sent(first(mg, SIDE - 1), mg_send)
     all_sent(first(q0, spots - 1), q_send.at[0])
     all_sent(first(q2, DEPTH - 1), q_send.at[1])
     all_sent(first(q3, spots - 1), q_send.at[2])
-    for h in range(2):
-        all_sent(summed.at[pl.ds(0, DEPTH - 1), :, :, halves[h]], sum_send.at[h])
+    for h in range(SIDE):
+        all_sent(summed.at[pl.ds(0, DEPTH - 1), :, :, pieces[h]], sum_send.at[h])
         pair_copy(h).wait_send()
     all_sent(first(leave, SIDE - 1), fin_send)
 
@@ -734,12 +696,11 @@
         vmem(spread[1:], bf16),
         vmem(spread[1:], bf16),
         vmem((EXPS, own, width), f32),
-        vmem((2, depth // 2, 2 * lanes), bf16),
         dma((9,)),
         dma,
         dma((3,)),
         dma,
-        dma((5,)),
+        dma((3,)),
         dma,
         dma,
         dma,
@@ -757,11 +718,11 @@
         dma((SIDE,)),
         dma((SIDE,)),
         dma,
-        dma((3,)),
-        dma((2,)),
-        dma((2,)),
-        dma((2,)),
-        dma((2,)),
+        dma,
+        dma((SIDE,)),
+        dma((SIDE,)),
+        dma((SIDE,)),
+        dma((SIDE,)),
         dma,
         dma,
     ]

time: 161 us -> 159 us (0.988)
  Pallas kernels: 160 us -> 158 us
    pallas_call x1, Pallas kernels: 160 us -> 158 us  [local(): pl.pallas_call(functools.partial(layer_kernel, len(scratch)), out_shape=j...]
where the time goes in v5:
time: 159 us
  Pallas kernels  158 us (99%)
    pallas_call x1, Pallas kernels, local(): pl.pallas_call(functools.partial(layer_kernel, len(scratch)), out_shape=j...  158 us

profile of v5, /device:TPU:1, one launch (start us, length us, event | category | flops | bytes accessed | tf_op | source)
XLA Modules:
  0.0 159.2 jit_solution(15696708477708205759)
XLA Ops:
  0.0 157.7 %layer.1 = bf16[8,4096]{1,0:T(8,128)(2,1)} custom-call(bf16[128,256]{1,0:T(8,128)(2,1)} %refs_0_.1, bf16[256,512]{1,0:T(8,128)(2,1)} %refs_1_.1, bf16[256,512]{1,0:T(8,128)(2,1)} %refs_2_.1, f32[4,512]{1,0:T(4,128)} %refs_3_.1, f32[1,512]{1,0:T(1,128)} %bitcast.15, bf16[32,512]{1,0:T(8,128)(2,1)} %bitcast.13, f32[128,512]{1,0:T(8,128)} %refs_6_.1, ...), custom_call_target="tpu_custom_call" | custom-call | tf_op jit(solution)/shard_map/layer/pallas_call | solution.py:1108
  157.7 1.5 copy.17
